TPU v7x, 256 devices: a whole 4x4x8 slice. The times are simulated.
256 devices in a mesh: feat: 16 (over x, y), layer: 4 (over z_lo), tok: 4 (over z_hi, core).
Axes of the slice: x: 4, y: 4, z: 8 (z_hi: 2, z_lo: 4; z = z_hi * 4 + z_lo), core: 2. Of those that a mesh axis runs over, the one named last changes fastest.
Arguments:
- captured: bfloat16 [4, 512, 2304], P('layer', 'tok', 'feat'), may hold values from -6 to 6
- target: bfloat16 [4, 512, 2304], P('layer', 'feat', 'tok'), may hold values from -6 to 6
- enc_weight: bfloat16 [4, 2304, 16384], P('layer', 'tok', 'feat'), may hold values from -0.125 to 0.125
- enc_bias: float32 [4, 16384], P('layer', 'feat'), may hold values from -3 to 3
- dec_weight: bfloat16 [4, 4, 16384, 2304], P('layer', None, 'feat', 'tok'), may hold values from -0.03125 to 0.03125
- dec_bias: float32 [4, 2304], P('layer', 'tok'), may hold values from -3 to 3
Outputs:
- enc_weight_grad: bfloat16 [4, 2304, 16384], P('layer', 'tok', 'feat')
- enc_bias_grad: float32 [4, 16384], P('layer', 'feat')
- dec_weight_grad: bfloat16 [4, 4, 16384, 2304], P('layer', None, 'feat', 'tok')
- dec_bias_grad: float32 [4, 2304], P('layer', 'tok')
All inputs are finite; a program needn't handle non-finite values.
Results may differ from a plain program's by a relative error of at most 0.008.
Values may be sent and summed in bfloat16 or wider, within the bound.
No kernel may reach another device: no remote copies, remote signals or barrier semaphores. Data moves between devices by JAX's collectives and lax.ppermute only.
A program may use at most 64 MiB of HBM per device.

v0:
```python
import math

import jax
import jax.numpy as jnp
from jax import lax
from jax.sharding import Mesh
from jax.sharding import PartitionSpec as P

FEAT = ("feat_0", "feat_1")


def in_order(pieces, dim):
    pieces = jnp.moveaxis(pieces, 0, dim)
    lengths = pieces.shape
    return pieces.reshape(*lengths[:dim], lengths[dim] * lengths[dim + 1], *lengths[dim + 2 :])


def sent_to_all(shard, axis):
    length = lax.axis_size(axis)
    return lax.all_to_all(
        jnp.broadcast_to(shard[None], (length, *shard.shape)), axis, 0, 0, tiled=True
    )


def gather_directly(shard, axis, dim):
    return in_order(sent_to_all(shard, axis), dim)


def split_up(shard, dim, length):
    before, after = (shard.shape[:dim], shard.shape[dim + 1 :])
    return jnp.moveaxis(shard.reshape(*before, length, -1, *after), dim, 0)


def summed_on_arrival(shard, axis, dim):
    length = lax.axis_size(axis)
    pieces = lax.all_to_all(split_up(shard, dim, length), axis, 0, 0, tiled=True)
    return jnp.sum(pieces, axis=0)


def one_axis_at_a_time(shard, axes):
    for axis in axes:
        shard = lax.psum(shard, axis)
    return shard


def contract_rows(left, right):
    return lax.dot_general(
        left, right, (((0,), (0,)), ((), ())), preferred_element_type=jnp.float32
    )


def on_device(captured, target, enc_weight, enc_bias, dec_weight, dec_bias):
    layer = lax.axis_index("layer")
    nlayer = dec_weight.shape[1]
    feat_cols = enc_weight.shape[2]
    width_part = enc_weight.shape[1]
    total_tokens = target.shape[1] * lax.axis_size(FEAT)
    scale = 1.0 / math.sqrt(total_tokens)
    encoder = enc_weight[0]
    rows = gather_directly(captured[0], FEAT, 1)
    moved = lax.all_to_all(rows, "tok", split_axis=1, concat_axis=0, tiled=True)
    block = moved
    pre = (
        summed_on_arrival(jnp.dot(block, encoder, preferred_element_type=jnp.float32), "tok", 0)
        + enc_bias
    )
    act = jnp.maximum(pre, 0.0).astype(jnp.bfloat16)
    act_all = gather_directly(act, "tok", 0)
    all_tokens = act_all.shape[0]

    def decode_step(write, partial_value):
        weight = lax.dynamic_index_in_dim(dec_weight[0], write, 0, keepdims=False)
        output = jnp.dot(act_all, weight, preferred_element_type=jnp.float32)
        return lax.dynamic_update_index_in_dim(partial_value, output, write, 0)

    partial_value = jnp.zeros((nlayer, all_tokens, width_part), jnp.float32)
    partial_value = lax.fori_loop(layer, nlayer, decode_step, partial_value)
    shared = summed_on_arrival(partial_value, "layer", 0)
    recon = summed_on_arrival(shared, FEAT, 1)
    err = recon + dec_bias[:, None, :] - target.astype(jnp.float32)
    scaled = err * scale
    dec_bias_grad = one_axis_at_a_time(jnp.sum(scaled, axis=1), FEAT)
    grad_out = scaled.astype(jnp.bfloat16)
    spread = gather_directly(grad_out, FEAT, 1)
    grad_all = gather_directly(spread, "layer", 0)

    def back_step(write, carry):
        dec_grads, grad_act = carry
        weight = lax.dynamic_index_in_dim(dec_weight[0], write, 0, keepdims=False)
        upstream = lax.dynamic_index_in_dim(grad_all, write, 0, keepdims=False)
        block = contract_rows(act_all, upstream).astype(jnp.bfloat16)
        dec_grads = lax.dynamic_update_index_in_dim(dec_grads, block, write, 0)
        grad_act = grad_act + lax.dot_general(
            upstream, weight, (((1,), (1,)), ((), ())), preferred_element_type=jnp.float32
        )
        return (dec_grads, grad_act)

    dec_start = jnp.zeros((nlayer, feat_cols, width_part), jnp.bfloat16)
    act_start = jnp.zeros((all_tokens, feat_cols), jnp.float32)
    dec_grads, grad_act = lax.fori_loop(layer, nlayer, back_step, (dec_start, act_start))
    grad_mine = summed_on_arrival(grad_act, "tok", 0)
    grad_pre = jnp.where(pre > 0, grad_mine, 0.0).astype(jnp.bfloat16)
    grad_every = gather_directly(grad_pre, "tok", 0)
    enc_bias_grad = jnp.sum(grad_every.astype(jnp.float32), axis=0)
    enc_grad = contract_rows(moved, grad_every)
    return (
        enc_grad.astype(jnp.bfloat16)[None],
        enc_bias_grad[None],
        dec_grads[None],
        dec_bias_grad,
    )


def solution(mesh):
    split = Mesh(
        mesh.devices.reshape(4, 4, mesh.shape["layer"], mesh.shape["tok"]),
        ("feat_0", "feat_1", "layer", "tok"),
    )
    return jax.shard_map(
        on_device,
        mesh=split,
        in_specs=(
            P("layer", "tok", FEAT),
            P("layer", FEAT, "tok"),
            P("layer", "tok", FEAT),
            P("layer", FEAT),
            P("layer", None, FEAT, "tok"),
            P("layer", "tok"),
        ),
        out_specs=(
            P("layer", "tok", FEAT),
            P("layer", FEAT),
            P("layer", None, FEAT, "tok"),
            P("layer", "tok"),
        ),
        check_vma=False,
    )
```

profile of v0, /device:TPU:1, one launch (start us, length us, event | category | flops | bytes accessed | tf_op | source)
XLA Modules:
  0.0 457.9 jit_solution(17982845756890526074)
XLA Ops:
  1.6 18.5 %all_to_all.61 = bf16[16,128,144]{1,2,0:T(8,128)(2,1)S(1)} all-to-all(bf16[16,128,144]{1,2,0:T(8,128)(2,1)S(1)} %broadcast_in_dim.64), channel_id=1, replica_groups=mesh['feat_0'=4,'feat_1'=4,'layer'=4,'tok'=4] {'feat_0','feat_1'}, dimensions={0} | all-to-all | bytes 1179648 | tf_op jit(solution)/shard_map/all_to_all | solution.py:20
  20.0 24.1 %all_to_all.62 = bf16[128,4,576]{0,2,1:T(8,128)(2,1)S(1)} all-to-all(bf16[128,4,576]{0,2,1:T(8,128)(2,1)S(1)} %bitcast.98), channel_id=1, replica_groups=mesh['feat_0'=4,'feat_1'=4,'layer'=4,'tok'=4] {'tok'}, dimensions={1} | all-to-all | bytes 1179648 | tf_op jit(solution)/shard_map/all_to_all | solution.py:61
  45.9 32.1 %all_to_all.63 = f32[4,128,1024]{2,1,0:T(8,128)S(1)} all-to-all(f32[4,128,1024]{2,1,0:T(8,128)S(1)} %fusion.15), channel_id=1, replica_groups=mesh['feat_0'=4,'feat_1'=4,'layer'=4,'tok'=4] {'tok'}, dimensions={0} | all-to-all | bytes 4194304 | tf_op jit(solution)/shard_map/all_to_all | solution.py:36
  81.2 26.8 %all-to-all-start.3 = ((bf16[4,128,1024]{2,1,0:T(8,128)(2,1)}), bf16[4,128,1024]{2,1,0:T(8,128)(2,1)S(1)}, u32[]{:S(2)}, u32[]{:S(2)}) async-start(bf16[4,128,1024]{2,1,0:T(8,128)(2,1)} %broadcast_in_dim.68), calls=%async_computation.3 | async-start | bytes 2097152 | tf_op jit(solution)/shard_map/all_to_all | solution.py:20
  108.0 17.5 %all-to-all-done.3 = bf16[4,128,1024]{2,1,0:T(8,128)(2,1)S(1)} async-done(((bf16[4,128,1024]{2,1,0:T(8,128)(2,1)}), bf16[4,128,1024]{2,1,0:T(8,128)(2,1)S(1)}, u32[]{:S(2)}, u32[]{:S(2)}) %all-to-all-start.3) | async-done | bytes 1048608 | tf_op jit(solution)/shard_map/all_to_all | solution.py:20
  128.3 12.4 %while.22 = (s32[]{:T(128)}, f32[4,512,576]{1,2,0:T(8,128)}, bf16[1,4,1024,576]{2,3,1,0:T(8,128)(2,1)}, bf16[512,1024]{1,0:T(8,128)(2,1)S(1)}, s32[]{:T(128)}, /*index=5*/s32[]{:T(128)}, s32[]{:T(128)}) while((s32[]{:T(128)}, f32[4,512,576]{1,2,0:T(8,128)}, bf16[1,4,1024,576]{2,3,1,0:T(8,128)(2,1)}, bf16[512,1024]{1,0:T(8,128)(2,1)S(1)}, ...), condition=%wide.region_2.3_spmd, body=%wide.region_1.2_spmd.sunk | while | flops 603979776 | bytes 3409015 | solution.py:77
  128.3 3.1 fusion.37
  131.4 3.1 fusion.37
  134.5 3.1 fusion.37
  137.6 3.1 fusion.37
  141.7 115.2 %all_to_all.64 = f32[4,1,512,576]{2,3,1,0:T(8,128)S(1)} all-to-all(f32[4,1,512,576]{2,3,1,0:T(8,128)} %bitcast.93), channel_id=1, replica_groups=mesh['feat_0'=4,'feat_1'=4,'layer'=4,'tok'=4] {'layer'}, dimensions={0} | all-to-all | bytes 9437184 | tf_op jit(solution)/shard_map/all_to_all | solution.py:36
  258.9 3.8 all-to-all-start.5
  262.8 18.2 %all-to-all-done.5 = f32[16,1,32,576]{3,2,1,0:T(8,128)S(1)} async-done(((f32[16,1,32,576]{3,2,1,0:T(8,128)}), f32[16,1,32,576]{3,2,1,0:T(8,128)S(1)}, u32[]{:S(2)}, u32[]{:S(2)}) %all-to-all-start.5) | async-done | bytes 1179680 | tf_op jit(solution)/shard_map/all_to_all | solution.py:36
  281.2 13.3 %all_to_all.65 = bf16[16,1,32,576]{3,2,1,0:T(8,128)(2,1)S(1)} all-to-all(bf16[16,1,32,576]{3,2,1,0:T(8,128)(2,1)S(1)} %broadcast_in_dim.70), channel_id=1, replica_groups=mesh['feat_0'=4,'feat_1'=4,'layer'=4,'tok'=4] {'feat_0','feat_1'}, dimensions={0} | all-to-all | bytes 1179648 | tf_op jit(solution)/shard_map/all_to_all | solution.py:20
  295.0 55.5 %all_to_all.66 = bf16[4,1,512,576]{2,3,1,0:T(8,128)(2,1)} all-to-all(bf16[4,1,512,576]{2,3,1,0:T(8,128)(2,1)S(1)} %broadcast_in_dim.72), channel_id=1, replica_groups=mesh['feat_0'=4,'feat_1'=4,'layer'=4,'tok'=4] {'layer'}, dimensions={0} | all-to-all | bytes 4718592 | tf_op jit(solution)/shard_map/all_to_all | solution.py:20
  353.5 21.9 %while.23 = (s32[]{:T(128)}, bf16[4,1024,576]{1,2,0:T(8,128)(2,1)}, f32[512,1024]{1,0:T(8,128)S(1)}, bf16[4,512,576]{1,2,0:T(8,128)(2,1)}, bf16[512,1024]{1,0:T(...) while((s32[]{:T(128)}, bf16[4,1024,576]{1,2,0:T(8,128)(2,1)}, ...), condition=%wide.region_6.7_spmd, body=%wide.region_5.6_spmd.sunk | while | flops 1209073664 | bytes 12978339 | solution.py:100
  356.1 2.9 fusion.42
  361.6 2.9 fusion.42
  367.0 2.9 fusion.42
  375.4 44.1 %all_to_all.67 = f32[4,128,1024]{2,1,0:T(8,128)} all-to-all(f32[4,128,1024]{2,1,0:T(8,128)S(1)} %bitcast.92), channel_id=1, replica_groups=mesh['feat_0'=4,'feat_1'=4,'layer'=4,'tok'=4] {'tok'}, dimensions={0} | all-to-all | bytes 4194304 | tf_op jit(solution)/shard_map/all_to_all | solution.py:36
  422.5 7.2 %all-to-all-start.9 = ((bf16[4,128,1024]{2,1,0:T(8,128)(2,1)}), bf16[4,128,1024]{2,1,0:T(8,128)(2,1)S(1)}, u32[]{:S(2)}, u32[]{:S(2)}) async-start(bf16[4,128,1024]{2,1,0:T(8,128)(2,1)} %broadcast_in_dim.73), calls=%async_computation.9 | async-start | bytes 2097152 | tf_op jit(solution)/shard_map/all_to_all | solution.py:20
  429.8 7.3 %psum.14 = f32[1,576]{1,0:T(1,128)S(1)} all-reduce(f32[1,576]{1,0:T(1,128)S(1)} %reduce_sum.65), channel_id=1, replica_groups=mesh['feat_0'=4,'feat_1'=4,'layer'=4,'tok'=4] {'feat_0'}, use_global_device_ids=true, to_apply=%region_10.11 | all-reduce | flops 576 | bytes 4608 | tf_op jit(solution)/shard_map/psum | solution.py:42
  437.1 7.7 %psum.15 = f32[1,576]{1,0:T(1,128)} all-reduce(f32[1,576]{1,0:T(1,128)S(1)} %psum.14), channel_id=1, replica_groups=mesh['feat_0'=4,'feat_1'=4,'layer'=4,'tok'=4] {'feat_1'}, use_global_device_ids=true, to_apply=%region_11.12 | all-reduce | flops 576 | bytes 4608 | tf_op jit(solution)/shard_map/psum | solution.py:42
  444.7 10.6 %all-to-all-done.9 = bf16[4,128,1024]{2,1,0:T(8,128)(2,1)S(1)} async-done(((bf16[4,128,1024]{2,1,0:T(8,128)(2,1)}), bf16[4,128,1024]{2,1,0:T(8,128)(2,1)S(1)}, u32[]{:S(2)}, u32[]{:S(2)}) %all-to-all-start.9) | async-done | bytes 1048608 | tf_op jit(solution)/shard_map/all_to_all | solution.py:20
  (51 shorter events, 34.2 us)
Async XLA Ops:
  0.6 44.3 %copy-start = (bf16[1,576,1024]{2,1,0:T(8,128)(2,1)S(1)}, bf16[1,576,1024]{2,1,0:T(8,128)(2,1)}, u32[]{:S(2)}) copy-start(bf16[1,576,1024]{2,1,0:T(8,128)(2,1)} %param.12) | copy-start | bytes 3538948
  44.1 0.8 copy-start.2
  78.0 1.0 copy-start.7
  81.2 44.3 %all-to-all-start.3 = ((bf16[4,128,1024]{2,1,0:T(8,128)(2,1)}), bf16[4,128,1024]{2,1,0:T(8,128)(2,1)S(1)}, u32[]{:S(2)}, u32[]{:S(2)}) async-start(bf16[4,128,1024]{2,1,0:T(8,128)(2,1)} %broadcast_in_dim.68), calls=%async_computation.3 | async-start | bytes 2097152 | tf_op jit(solution)/shard_map/all_to_all | solution.py:20
  140.7 1.0 copy-start.4
  257.5 5.3 %copy-start.8 = (f32[1,576]{1,0:T(1,128)S(1)}, f32[1,576]{1,0:T(1,128)}, u32[]{:S(2)}) copy-start(f32[1,576]{1,0:T(1,128)} %param.15) | copy-start | bytes 6916
  258.9 22.2 %copy-start.6 = (bf16[1,32,576]{2,1,0:T(8,128)(2,1)S(1)}, bf16[1,32,576]{2,1,0:T(8,128)(2,1)}, u32[]{:S(2)}) copy-start(bf16[1,32,576]{2,1,0:T(8,128)(2,1)} %param.11) | copy-start | bytes 110596
  258.9 22.1 %all-to-all-start.5 = ((f32[16,1,32,576]{3,2,1,0:T(8,128)}), f32[16,1,32,576]{3,2,1,0:T(8,128)S(1)}, u32[]{:S(2)}, u32[]{:S(2)}) async-start(f32[16,1,32,576]{3,2,1,0:T(8,128)} %bitcast.95), calls=%async_computation.5 | async-start | bytes 2621440 | tf_op jit(solution)/shard_map/all_to_all | solution.py:36
  353.5 2.6 copy-start.5
  359.0 2.6 copy-start.5
  364.4 2.6 copy-start.5
  369.9 2.6 copy-start.5
  419.4 1.9 copy-start.1
  421.4 34.7 %copy-start.3 = (bf16[128,4,576]{0,2,1:T(8,128)(2,1)S(1)}, bf16[128,4,576]{0,2,1:T(8,128)(2,1)}, u32[]{:S(2)}) copy-start(bf16[128,4,576]{0,2,1:T(8,128)(2,1)} %copy-done.2) | copy-start | bytes 1769476
  422.5 32.8 %all-to-all-start.9 = ((bf16[4,128,1024]{2,1,0:T(8,128)(2,1)}), bf16[4,128,1024]{2,1,0:T(8,128)(2,1)S(1)}, u32[]{:S(2)}, u32[]{:S(2)}) async-start(bf16[4,128,1024]{2,1,0:T(8,128)(2,1)} %broadcast_in_dim.73), calls=%async_computation.9 | async-start | bytes 2097152 | tf_op jit(solution)/shard_map/all_to_all | solution.py:20
where the time goes:
time: 459 us; the launch traced here: 458 us
  blocking collectives  318 us (69%)
  waiting for transfers between devices  46.4 us (10%)
  starting transfers between devices  37.9 us (8%)
  matrix products  36.9 us (8%)
  local copies, waits for them, and re-layouts  12.7 us (3%)
  other arithmetic  5.49 us (1%)
    all_to_all x3, blocking collectives, summed_on_arrival(): lax.all_to_all(split_up(shard, dim, length), axis, 0, 0, tiled=True)  191 us
    all_to_all x3, blocking collectives, sent_to_all(): lax.all_to_all(jnp.broadcast_to(shard[None], (length, *shard.shape)), axi...  87.2 us
    all_to_all x2, starting transfers between devices, sent_to_all(): lax.all_to_all(jnp.broadcast_to(shard[None], (length, *shard.shape)), axi...  34 us
    all_to_all x2, waiting for transfers between devices, sent_to_all(): lax.all_to_all(jnp.broadcast_to(shard[None], (length, *shard.shape)), axi...  28.2 us
    all_to_all x1, blocking collectives, on_device(): moved = lax.all_to_all(rows, 'tok', split_axis=1, concat_axis=0, tiled=True)  24.1 us
    all_to_all x1, waiting for transfers between devices, summed_on_arrival(): lax.all_to_all(split_up(shard, dim, length), axis, 0, 0, tiled=True)  18.2 us
    psum x2, blocking collectives, one_axis_at_a_time(): shard = lax.psum(shard, axis)  14.9 us
    dot_general x5, matrix products, contract_rows(): lax.dot_general(left, right, (((0,), (0,)), ((), ())), preferred_element_...  13.3 us
  transfers between devices with their start and end apart: 3, of which 3 were waited for; matrix products, arithmetic and copies ran while one was open for 0% of the time, Pallas kernels for 0%

commit v1 on v0

v1 whole, which is shorter than its diff:
```python
import math

import jax
import jax.numpy as jnp
from jax import lax
from jax.sharding import Mesh
from jax.sharding import PartitionSpec as P

FEAT = ("x", "y")
TOK = ("half", "core")


def swapped(value, axis):
    return lax.ppermute(value, axis, [(0, 1), (1, 0)])


def both(own, other, index, dim):
    first = jnp.where(index == 0, own, other)
    second = jnp.where(index == 0, other, own)
    return jnp.concatenate([first, second], axis=dim)


def sent_to_all(shard, axis):
    length = lax.axis_size(axis)
    return lax.all_to_all(
        jnp.broadcast_to(shard[None], (length, *shard.shape)), axis, 0, 0, tiled=True
    )


def dot(left, right, left_dim, right_dim):
    return lax.dot_general(
        left,
        right,
        (((left_dim,), (right_dim,)), ((), ())),
        preferred_element_type=jnp.float32,
    )


def on_device(captured, target, enc_weight, enc_bias, dec_weight, dec_bias):
    layer = lax.axis_index("layer")
    half = lax.axis_index("half")
    core = lax.axis_index("core")
    nlayer = dec_weight.shape[1]
    width = enc_weight.shape[1]
    feats = enc_weight.shape[2]
    rows = captured.shape[1]
    nfeat = lax.axis_size(FEAT)
    tokens = rows * lax.axis_size(TOK)
    scale = 1.0 / math.sqrt(tokens)
    encoder = enc_weight[0]
    decoder = dec_weight[0]

    cols = feats // 2
    mine = lax.dynamic_slice_in_dim(encoder, half * cols, cols, 1)
    theirs = lax.dynamic_slice_in_dim(encoder, (1 - half) * cols, cols, 1)
    crossed = swapped(theirs, "half")
    mine_next = swapped(mine, "core")
    small = captured[0].T
    small = both(small, swapped(small, "half"), half, 1)
    wide = sent_to_all(small, FEAT)
    wide = wide.reshape(-1, wide.shape[2])
    crossed_next = swapped(crossed, "core")

    def block(h, c):
        return lax.dynamic_slice_in_dim(wide, (h * 2 + c) * width, width, 0)

    pre = dot(block(half, core), mine, 0, 0)
    pre = pre + dot(block(half, 1 - core), mine_next, 0, 0)
    pre = pre + dot(block(1 - half, core), crossed, 0, 0)
    pre = pre + dot(block(1 - half, 1 - core), crossed_next, 0, 0)
    pre = pre + lax.dynamic_slice_in_dim(enc_bias, half * cols, cols, 1)
    act = jnp.maximum(pre, 0.0).astype(jnp.bfloat16)
    act = both(act, swapped(act, "half"), half, 1)
    pair = both(act[None], swapped(act, "core")[None], core, 0)
    act_all = pair.reshape(2, 2, rows, feats).swapaxes(0, 1).reshape(tokens, feats)

    moved = block(half, core)
    moved_next = swapped(block(half, 1 - core), "core")
    moved = both(moved[:, None], moved_next[:, None], core, 1)
    moved = moved.reshape(width, 2, 2, rows).swapaxes(1, 2).reshape(width, tokens)

    offset = dec_bias[0][None, :] - target[0].astype(jnp.float32)
    grads = [None] * nlayer
    for write in reversed(range(nlayer)):
        partial = dot(act_all, decoder[write], 1, 0).astype(jnp.bfloat16)
        partial = partial.reshape(nfeat, tokens // nfeat, width)
        pieces = lax.all_to_all(partial, FEAT, 0, 0, tiled=True)
        recon = jnp.sum(pieces.astype(jnp.float32), axis=0)
        recon = recon + jnp.where(layer == write, offset, 0.0)
        shared = recon.astype(jnp.bfloat16)
        for step in range(1, write + 1):
            ring = [(k, (k + step) % (write + 1)) for k in range(write + 1)]
            recon = recon + lax.ppermute(shared, "layer", ring).astype(jnp.float32)
        scaled = recon * scale
        grad = jnp.where(write >= layer, scaled, 0.0).astype(jnp.bfloat16)
        grads[write] = sent_to_all(grad, FEAT).reshape(tokens, width)

    dec_grads = jnp.zeros((nlayer, feats, width), jnp.bfloat16)
    grad_act = None
    for write in reversed(range(nlayer)):
        term = dot(grads[write], decoder[write], 1, 1)
        grad_act = term if grad_act is None else grad_act + term
    for write in reversed(range(nlayer)):
        block_grad = dot(act_all, grads[write], 0, 0).astype(jnp.bfloat16)
        dec_grads = lax.dynamic_update_index_in_dim(dec_grads, block_grad, write, 0)
    own = lax.dynamic_index_in_dim(jnp.stack(grads), layer, 0, keepdims=False)
    dec_bias_grad = jnp.sum(own.astype(jnp.float32), axis=0)

    few = tokens // 2
    keep = lax.dynamic_slice_in_dim(grad_act, core * few, few, 0)
    give = lax.dynamic_slice_in_dim(grad_act, (1 - core) * few, few, 0)
    keep = keep + swapped(give.astype(jnp.bfloat16), "core").astype(jnp.float32)
    keep = lax.optimization_barrier(keep.astype(jnp.bfloat16))
    grad_mine = keep.astype(jnp.float32) + swapped(keep, "half").astype(jnp.float32)
    act_mine = lax.dynamic_slice_in_dim(act_all, core * few, few, 0)
    grad_pre = jnp.where(act_mine > 0, grad_mine, 0.0).astype(jnp.bfloat16)
    grad_every = both(grad_pre, swapped(grad_pre, "core"), core, 0)
    enc_bias_grad = jnp.sum(grad_every.astype(jnp.float32), axis=0)
    enc_grad = dot(moved, grad_every, 1, 0).astype(jnp.bfloat16)
    return (enc_grad[None], enc_bias_grad[None], dec_grads[None], dec_bias_grad[None])


def solution(mesh):
    split = Mesh(
        mesh.devices.reshape(4, 4, mesh.shape["layer"], 2, 2),
        ("x", "y", "layer", "half", "core"),
    )
    return jax.shard_map(
        on_device,
        mesh=split,
        in_specs=(
            P("layer", TOK, FEAT),
            P("layer", FEAT, TOK),
            P("layer", TOK, FEAT),
            P("layer", FEAT),
            P("layer", None, FEAT, TOK),
            P("layer", TOK),
        ),
        out_specs=(
            P("layer", TOK, FEAT),
            P("layer", FEAT),
            P("layer", None, FEAT, TOK),
            P("layer", TOK),
        ),
        check_vma=False,
    )
```

time: 459 us -> 284 us (0.62)
  blocking collectives: 318 us -> 15.9 us
  starting transfers between devices: 37.9 us -> 112 us
  waiting for transfers between devices: 46.4 us -> 77.2 us
  local copies, waits for them, and re-layouts: 12.7 us -> 30.6 us
    all_to_all x4 -> x0, blocking collectives: 215 us -> none  [the longest x3 191 us: summed_on_arrival(): lax.all_to_all(split_up(shard, dim, length), axis, 0, 0, tiled=True)]
    ppermute x0 -> x16, starting transfers between devices: none -> 73.2 us  [the longest x10 57.4 us: swapped(): return lax.ppermute(value, axis, [(0, 1), (1, 0)])]
    all_to_all x3 -> x1, blocking collectives: 87.2 us -> 15.9 us  [sent_to_all(): lax.all_to_all(jnp.broadcast_to(shard[None], (length, *shard.shape)), axi...]
    ppermute x0 -> x16, waiting for transfers between devices: none -> 49.1 us  [the longest x10 45.7 us: swapped(): return lax.ppermute(value, axis, [(0, 1), (1, 0)])]
    all_to_all x2 -> x4, waiting for transfers between devices: 28.2 us -> 10.5 us  [sent_to_all(): lax.all_to_all(jnp.broadcast_to(shard[None], (length, *shard.shape)), axi...]
    all_to_all x1 -> x4, starting transfers between devices: 3.83 us -> 19.8 us  [on_device(): pieces = lax.all_to_all(partial, FEAT, 0, 0, tiled=True)]
    all_to_all x2 -> x4, starting transfers between devices: 34 us -> 18.5 us  [sent_to_all(): lax.all_to_all(jnp.broadcast_to(shard[None], (length, *shard.shape)), axi...]
    psum x2 -> x0, blocking collectives: 14.9 us -> none  [one_axis_at_a_time(): shard = lax.psum(shard, axis)]
  transfers between devices with their start and end apart: 3 -> 24, of which waited for: 3 -> 14; matrix products, arithmetic and copies ran while one was open for 0% -> 22% of each run, Pallas kernels for 0% -> 0%
where the time goes in v1:
time: 284 us; the launch traced here: 282 us
  starting transfers between devices  112 us (39%)
  waiting for transfers between devices  77.2 us (27%)
  matrix products  36 us (13%)
  local copies, waits for them, and re-layouts  30.6 us (11%)
  blocking collectives  15.9 us (6%)
  other arithmetic  9.57 us (3%)
    ppermute x10, starting transfers between devices, swapped(): return lax.ppermute(value, axis, [(0, 1), (1, 0)])  57.4 us
    ppermute x10, waiting for transfers between devices, swapped(): return lax.ppermute(value, axis, [(0, 1), (1, 0)])  45.7 us
    dot_general x17, matrix products, dot(): lax.dot_general(left, right, (((left_dim,), (right_dim,)), ((), ())), pre...  36 us
    all_to_all x4, starting transfers between devices, on_device(): pieces = lax.all_to_all(partial, FEAT, 0, 0, tiled=True)  19.8 us
    all_to_all x4, starting transfers between devices, sent_to_all(): lax.all_to_all(jnp.broadcast_to(shard[None], (length, *shard.shape)), axi...  18.5 us
    all_to_all x4, waiting for transfers between devices, on_device(): pieces = lax.all_to_all(partial, FEAT, 0, 0, tiled=True)  17.5 us
    all_to_all x1, blocking collectives, sent_to_all(): lax.all_to_all(jnp.broadcast_to(shard[None], (length, *shard.shape)), axi...  15.9 us
    ppermute x6, starting transfers between devices, on_device(): recon = recon + lax.ppermute(shared, 'layer', ring).astype(jnp.float32)  15.9 us
  transfers between devices with their start and end apart: 24, of which 14 were waited for; matrix products, arithmetic and copies ran while one was open for 22% of the time, Pallas kernels for 0%

profile of v1, /device:TPU:1, one launch (start us, length us, event | category | flops | bytes accessed | tf_op | source)
XLA Modules:
  0.0 282.0 jit_solution(917064107540070880)
XLA Ops:
  0.7 7.8 %collective-permute-start = (bf16[144,128]{1,0:T(8,128)(2,1)}, bf16[144,128]{1,0:T(8,128)(2,1)S(1)}, u32[]{:S(2)}, u32[]{:S(2)}) collective-permute-start(bf16[144,128]{1,0:T(8,128)(2,1)} %bitcast.151), channel_id=1, source_target_pairs={{0,2},{2,0},{1,3},{3,1},{4,6},{6,4},{5,7},{7,5},{8,10},{10,8},{9,1... | collective-permute-start | bytes 110600 | tf_op jit(solution)/shard_map/ppermute | solution.py:14
  11.9 6.8 %all-to-all-start = ((bf16[16,144,256]{2,1,0:T(8,128)(2,1)}), bf16[16,144,256]{2,1,0:T(8,128)(2,1)S(1)}, u32[]{:S(2)}, u32[]{:S(2)}) async-start(bf16[16,144,256]{2,1,0:T(8,128)(2,1)} %broadcast_in_dim.79), calls=%async_computation | async-start | bytes 2359296 | tf_op jit(solution)/shard_map/all_to_all | solution.py:25
  19.6 5.8 %collective-permute-start.3 = (bf16[576,512]{1,0:T(8,128)(2,1)}, bf16[576,512]{1,0:T(8,128)(2,1)S(1)}, u32[]{:S(2)}, u32[]{:S(2)}) collective-permute-start(bf16[576,512]{1,0:T(8,128)(2,1)} %get-tuple-element.6), channel_id=1, source_target_pairs={{0,2},{2,0},{1,3},{3,1},{4,6},{6,4},{5,7},{7,5},{8,10},{10,8},{9,1... | collective-permute-start | bytes 1769480 | tf_op jit(solution)/shard_map/ppermute | solution.py:14
  27.4 13.1 %collective-permute-done.3 = bf16[576,512]{1,0:T(8,128)(2,1)S(1)} collective-permute-done((bf16[576,512]{1,0:T(8,128)(2,1)}, bf16[576,512]{1,0:T(8,128)(2,1)S(1)}, u32[]{:S(2)}, u32[]{:S(2)}) %collective-permute-start.3) | collective-permute-done | bytes 589856 | tf_op jit(solution)/shard_map/ppermute | solution.py:14
  40.5 4.0 %collective-permute-start.4 = (bf16[576,512]{1,0:T(8,128)(2,1)S(1)}, bf16[576,512]{1,0:T(8,128)(2,1)S(1)}, u32[]{:S(2)}, u32[]{:S(2)}) collective-permute-start(bf16[576,512]{1,0:T(8,128)(2,1)S(1)} %collective-permute-done.3), channel_id=1, source_target_pairs={{0,1},{1,0},{2,3},{3,2},{4,5},{5,4},{6,7},{7,6},{8,9},{9,8},{10,11... | collective-permute-start | bytes 1769480 | tf_op jit(solution)/shard_map/ppermute | solution.py:14
  47.8 12.5 %collective-permute-start.5 = (bf16[256,512]{1,0:T(8,128)(2,1)S(1)}, bf16[256,512]{1,0:T(8,128)(2,1)S(1)}, u32[]{:S(2)}, u32[]{:S(2)}) collective-permute-start(bf16[256,512]{1,0:T(8,128)(2,1)S(1)} %fusion.10), channel_id=1, source_target_pairs={{0,2},{2,0},{1,3},{3,1},{4,6},{6,4},{5,7},{7,5},{8,10},{10,8},{9,1... | collective-permute-start | bytes 786440 | tf_op jit(solution)/shard_map/ppermute | solution.py:14
  60.4 7.3 %collective-permute-done.5 = bf16[256,512]{1,0:T(8,128)(2,1)S(1)} collective-permute-done((bf16[256,512]{1,0:T(8,128)(2,1)S(1)}, bf16[256,512]{1,0:T(8,128)(2,1)S(1)}, u32[]{:S(2)}, u32[]{:S(2)}) %collective-permute-start.5) | collective-permute-done | bytes 262176 | tf_op jit(solution)/shard_map/ppermute | solution.py:14
  74.1 6.6 %all-to-all-start.5 = ((bf16[16,32,576]{2,1,0:T(8,128)(2,1)}), bf16[16,32,576]{2,1,0:T(8,128)(2,1)S(1)}, u32[]{:S(2)}, u32[]{:S(2)}) async-start(bf16[16,32,576]{2,1,0:T(8,128)(2,1)} %bitcast.20), calls=%async_computation.5 | async-start | bytes 1310720 | tf_op jit(solution)/shard_map/all_to_all | solution.py:87
  83.9 8.2 %all-to-all-done.5 = bf16[16,32,576]{2,1,0:T(8,128)(2,1)S(1)} async-done(((bf16[16,32,576]{2,1,0:T(8,128)(2,1)}), bf16[16,32,576]{2,1,0:T(8,128)(2,1)S(1)}, u32[]{:S(2)}, u32[]{:S(2)}) %all-to-all-start.5) | async-done | bytes 589856 | tf_op jit(solution)/shard_map/all_to_all | solution.py:87
  92.2 4.1 %all-to-all-start.3 = ((bf16[16,32,576]{2,1,0:T(8,128)(2,1)}), bf16[16,32,576]{2,1,0:T(8,128)(2,1)S(1)}, u32[]{:S(2)}, u32[]{:S(2)}) async-start(bf16[16,32,576]{2,1,0:T(8,128)(2,1)} %bitcast.17), calls=%async_computation.3 | async-start | bytes 1310720 | tf_op jit(solution)/shard_map/all_to_all | solution.py:87
  101.4 4.7 %all-to-all-done.3 = bf16[16,32,576]{2,1,0:T(8,128)(2,1)S(1)} async-done(((bf16[16,32,576]{2,1,0:T(8,128)(2,1)}), bf16[16,32,576]{2,1,0:T(8,128)(2,1)S(1)}, u32[]{:S(2)}, u32[]{:S(2)}) %all-to-all-start.3) | async-done | bytes 589856 | tf_op jit(solution)/shard_map/all_to_all | solution.py:87
  106.1 5.1 %all-to-all-start.1 = ((bf16[16,32,576]{2,1,0:T(8,128)(2,1)}), bf16[16,32,576]{2,1,0:T(8,128)(2,1)S(1)}, u32[]{:S(2)}, u32[]{:S(2)}) async-start(bf16[16,32,576]{2,1,0:T(8,128)(2,1)} %bitcast.139), calls=%async_computation.1 | async-start | bytes 1310720 | tf_op jit(solution)/shard_map/all_to_all | solution.py:87
  116.8 4.6 %all-to-all-done.1 = bf16[16,32,576]{2,1,0:T(8,128)(2,1)S(1)} async-done(((bf16[16,32,576]{2,1,0:T(8,128)(2,1)}), bf16[16,32,576]{2,1,0:T(8,128)(2,1)S(1)}, u32[]{:S(2)}, u32[]{:S(2)}) %all-to-all-start.1) | async-done | bytes 589856 | tf_op jit(solution)/shard_map/all_to_all | solution.py:87
  121.4 4.0 %all-to-all-start.7 = ((bf16[16,32,576]{2,1,0:T(8,128)(2,1)}), bf16[16,32,576]{2,1,0:T(8,128)(2,1)S(1)}, u32[]{:S(2)}, u32[]{:S(2)}) async-start(bf16[16,32,576]{2,1,0:T(8,128)(2,1)} %bitcast.23), calls=%async_computation.7 | async-start | bytes 1310720 | tf_op jit(solution)/shard_map/all_to_all | solution.py:87
  125.6 8.1 %collective-permute-start.12 = (bf16[32,576]{1,0:T(8,128)(2,1)S(1)}, bf16[32,576]{1,0:T(8,128)(2,1)S(1)}, u32[]{:S(2)}, u32[]{:S(2)}) collective-permute-start(bf16[32,576]{1,0:T(8,128)(2,1)S(1)} %get-tuple-element.20), channel_id=1, source_target_pairs={{0,4},{4,0},{1,5},{5,1},{2,6},{6,2},{3,7},{7,3},{16,20},{20,16},{1... | collective-permute-start | bytes 110600 | tf_op jit(solution)/shard_map/ppermute | solution.py:93
  145.1 15.9 %all_to_all.45 = bf16[16,32,576]{2,1,0:T(8,128)(2,1)S(1)} all-to-all(bf16[16,32,576]{2,1,0:T(8,128)(2,1)S(1)} %broadcast_in_dim.82), channel_id=1, replica_groups=mesh['x'=4,'y'=4,'layer'=4,'half'=2,'core'=2] {'x','y'}, dimensions={0} | all-to-all | bytes 1179648 | tf_op jit(solution)/shard_map/all_to_all | solution.py:25
  165.6 7.2 %collective-permute-start.1 = (bf16[576,256]{1,0:T(8,128)(2,1)}, bf16[576,256]{1,0:T(8,128)(2,1)}, u32[]{:S(2)}, u32[]{:S(2)}) collective-permute-start(bf16[576,256]{1,0:T(8,128)(2,1)} %constant_dynamic-slice_fusion.1), channel_id=1, source_target_pairs={{0,1},{1,0},{2,3},{3,2},{4,5},{5,4},{6,7},{7,6},{8,9},{9,8},{10,11... | collective-permute-start | bytes 884744 | tf_op jit(solution)/shard_map/ppermute | solution.py:14
  176.1 4.5 %all-to-all-start.6 = ((bf16[16,32,576]{2,1,0:T(8,128)(2,1)}), bf16[16,32,576]{2,1,0:T(8,128)(2,1)}, u32[]{:S(2)}, u32[]{:S(2)}) async-start(bf16[16,32,576]{2,1,0:T(8,128)(2,1)} %broadcast_in_dim.83), calls=%async_computation.6 | async-start | bytes 1310720 | tf_op jit(solution)/shard_map/all_to_all | solution.py:25
  184.4 5.9 %all-to-all-done.6 = bf16[16,32,576]{2,1,0:T(8,128)(2,1)} async-done(((bf16[16,32,576]{2,1,0:T(8,128)(2,1)}), bf16[16,32,576]{2,1,0:T(8,128)(2,1)}, u32[]{:S(2)}, u32[]{:S(2)}) %all-to-all-start.6) | async-done | bytes 589856 | tf_op jit(solution)/shard_map/all_to_all | solution.py:25
  194.9 3.8 %fusion.13 = f32[512,1024]{1,0:T(8,128)} fusion(bf16[512,576]{1,0:T(8,128)(2,1)} %bitcast.21, bf16[1,4,1024,576]{2,3,1,0:T(8,128)(2,1)} %param.10), kind=kOutput, calls=%fused_computation.36 | convolution fusion | flops 603979776 | bytes 3932160 | tf_op jit(solution)/shard_map/dot_general | solution.py:31
  205.4 4.4 %add_add_fusion = f32[512,1024]{1,0:T(8,128)S(1)} fusion(f32[512,1024]{1,0:T(8,128)} %fusion.13, f32[512,1024]{1,0:T(8,128)} %fusion.19, f32[512,1024]{1,0:T(8,128)} %fusion.16, bf16[512,576]{1,0:T(8,128)(2,1)} %bitcast.130, bf16[1,4,1024,576]{2,3,1,0:T(8,128)(2,1)} %param.10), kind=kOutput, calls=%fused_computation.6 | convolution fusion | flops 605552640 | bytes 10223616 | tf_op jit(solution)/shard_map/dot_general | solution.py:31
  210.7 10.4 %collective-permute-start.13 = (bf16[256,1024]{1,0:T(8,128)(2,1)}, bf16[256,1024]{1,0:T(8,128)(2,1)}, u32[]{:S(2)}, u32[]{:S(2)}) collective-permute-start(bf16[256,1024]{1,0:T(8,128)(2,1)} %dynamic-slice_convert_fusion), channel_id=1, source_target_pairs={{0,1},{1,0},{2,3},{3,2},{4,5},{5,4},{6,7},{7,6},{8,9},{9,8},{10,11... | collective-permute-start | bytes 1572872 | tf_op jit(solution)/shard_map/ppermute | solution.py:14
  245.2 6.1 %collective-permute-start.14 = (bf16[256,1024]{1,0:T(8,128)(2,1)S(1)}, bf16[256,1024]{1,0:T(8,128)(2,1)S(1)}, u32[]{:S(2)}, u32[]{:S(2)}) collective-permute-start(bf16[256,1024]{1,0:T(8,128)(2,1)S(1)} %add_convert_fusion), channel_id=1, source_target_pairs={{0,2},{2,0},{1,3},{3,1},{4,6},{6,4},{5,7},{7,5},{8,10},{10,8},{9,1... | collective-permute-start | bytes 1572872 | tf_op jit(solution)/shard_map/ppermute | solution.py:14
  252.7 22.2 %collective-permute-done.14 = bf16[256,1024]{1,0:T(8,128)(2,1)S(1)} collective-permute-done((bf16[256,1024]{1,0:T(8,128)(2,1)S(1)}, bf16[256,1024]{1,0:T(8,128)(2,1)S(1)}, u32[]{:S(2)}, u32[]{:S(2)}) %collective-permute-start.14) | collective-permute-done | bytes 524320 | tf_op jit(solution)/shard_map/ppermute | solution.py:14
  (113 shorter events, 97.6 us)
Async XLA Ops:
  0.7 9.4 %collective-permute-start = (bf16[144,128]{1,0:T(8,128)(2,1)}, bf16[144,128]{1,0:T(8,128)(2,1)S(1)}, u32[]{:S(2)}, u32[]{:S(2)}) collective-permute-start(bf16[144,128]{1,0:T(8,128)(2,1)} %bitcast.151), channel_id=1, source_target_pairs={{0,2},{2,0},{1,3},{3,1},{4,6},{6,4},{5,7},{7,5},{8,10},{10,8},{9,1... | collective-permute-start | bytes 110600 | tf_op jit(solution)/shard_map/ppermute | solution.py:14
  11.9 32.6 %all-to-all-start = ((bf16[16,144,256]{2,1,0:T(8,128)(2,1)}), bf16[16,144,256]{2,1,0:T(8,128)(2,1)S(1)}, u32[]{:S(2)}, u32[]{:S(2)}) async-start(bf16[16,144,256]{2,1,0:T(8,128)(2,1)} %broadcast_in_dim.79), calls=%async_computation | async-start | bytes 2359296 | tf_op jit(solution)/shard_map/all_to_all | solution.py:25
  19.6 20.9 %collective-permute-start.3 = (bf16[576,512]{1,0:T(8,128)(2,1)}, bf16[576,512]{1,0:T(8,128)(2,1)S(1)}, u32[]{:S(2)}, u32[]{:S(2)}) collective-permute-start(bf16[576,512]{1,0:T(8,128)(2,1)} %get-tuple-element.6), channel_id=1, source_target_pairs={{0,2},{2,0},{1,3},{3,1},{4,6},{6,4},{5,7},{7,5},{8,10},{10,8},{9,1... | collective-permute-start | bytes 1769480 | tf_op jit(solution)/shard_map/ppermute | solution.py:14
  25.4 20.3 %collective-permute-start.2 = (bf16[576,512]{1,0:T(8,128)(2,1)S(1)}, bf16[576,512]{1,0:T(8,128)(2,1)S(1)}, u32[]{:S(2)}, u32[]{:S(2)}) collective-permute-start(bf16[576,512]{1,0:T(8,128)(2,1)S(1)} %get-tuple-element.7), channel_id=1, source_target_pairs={{0,1},{1,0},{2,3},{3,2},{4,5},{5,4},{6,7},{7,6},{8,9},{9,8},{10,11... | collective-permute-start | bytes 1769480 | tf_op jit(solution)/shard_map/ppermute | solution.py:14
  40.5 6.9 %collective-permute-start.4 = (bf16[576,512]{1,0:T(8,128)(2,1)S(1)}, bf16[576,512]{1,0:T(8,128)(2,1)S(1)}, u32[]{:S(2)}, u32[]{:S(2)}) collective-permute-start(bf16[576,512]{1,0:T(8,128)(2,1)S(1)} %collective-permute-done.3), channel_id=1, source_target_pairs={{0,1},{1,0},{2,3},{3,2},{4,5},{5,4},{6,7},{7,6},{8,9},{9,8},{10,11... | collective-permute-start | bytes 1769480 | tf_op jit(solution)/shard_map/ppermute | solution.py:14
  47.8 19.8 %collective-permute-start.5 = (bf16[256,512]{1,0:T(8,128)(2,1)S(1)}, bf16[256,512]{1,0:T(8,128)(2,1)S(1)}, u32[]{:S(2)}, u32[]{:S(2)}) collective-permute-start(bf16[256,512]{1,0:T(8,128)(2,1)S(1)} %fusion.10), channel_id=1, source_target_pairs={{0,2},{2,0},{1,3},{3,1},{4,6},{6,4},{5,7},{7,5},{8,10},{10,8},{9,1... | collective-permute-start | bytes 786440 | tf_op jit(solution)/shard_map/ppermute | solution.py:14
  67.7 2.3 collective-permute-start.6
  74.1 18.1 %all-to-all-start.5 = ((bf16[16,32,576]{2,1,0:T(8,128)(2,1)}), bf16[16,32,576]{2,1,0:T(8,128)(2,1)S(1)}, u32[]{:S(2)}, u32[]{:S(2)}) async-start(bf16[16,32,576]{2,1,0:T(8,128)(2,1)} %bitcast.20), calls=%async_computation.5 | async-start | bytes 1310720 | tf_op jit(solution)/shard_map/all_to_all | solution.py:87
  92.2 13.9 %all-to-all-start.3 = ((bf16[16,32,576]{2,1,0:T(8,128)(2,1)}), bf16[16,32,576]{2,1,0:T(8,128)(2,1)S(1)}, u32[]{:S(2)}, u32[]{:S(2)}) async-start(bf16[16,32,576]{2,1,0:T(8,128)(2,1)} %bitcast.17), calls=%async_computation.3 | async-start | bytes 1310720 | tf_op jit(solution)/shard_map/all_to_all | solution.py:87
  106.1 15.3 %all-to-all-start.1 = ((bf16[16,32,576]{2,1,0:T(8,128)(2,1)}), bf16[16,32,576]{2,1,0:T(8,128)(2,1)S(1)}, u32[]{:S(2)}, u32[]{:S(2)}) async-start(bf16[16,32,576]{2,1,0:T(8,128)(2,1)} %bitcast.139), calls=%async_computation.1 | async-start | bytes 1310720 | tf_op jit(solution)/shard_map/all_to_all | solution.py:87
  121.4 23.7 %all-to-all-start.7 = ((bf16[16,32,576]{2,1,0:T(8,128)(2,1)}), bf16[16,32,576]{2,1,0:T(8,128)(2,1)S(1)}, u32[]{:S(2)}, u32[]{:S(2)}) async-start(bf16[16,32,576]{2,1,0:T(8,128)(2,1)} %bitcast.23), calls=%async_computation.7 | async-start | bytes 1310720 | tf_op jit(solution)/shard_map/all_to_all | solution.py:87
  125.6 14.7 %collective-permute-start.12 = (bf16[32,576]{1,0:T(8,128)(2,1)S(1)}, bf16[32,576]{1,0:T(8,128)(2,1)S(1)}, u32[]{:S(2)}, u32[]{:S(2)}) collective-permute-start(bf16[32,576]{1,0:T(8,128)(2,1)S(1)} %get-tuple-element.20), channel_id=1, source_target_pairs={{0,4},{4,0},{1,5},{5,1},{2,6},{6,2},{3,7},{7,3},{16,20},{20,16},{1... | collective-permute-start | bytes 110600 | tf_op jit(solution)/shard_map/ppermute | solution.py:93
  133.7 7.8 %collective-permute-start.11 = (bf16[32,576]{1,0:T(8,128)(2,1)S(1)}, bf16[32,576]{1,0:T(8,128)(2,1)S(1)}, u32[]{:S(2)}, u32[]{:S(2)}) collective-permute-start(bf16[32,576]{1,0:T(8,128)(2,1)S(1)} %get-tuple-element.19), channel_id=1, source_target_pairs={{0,8},{4,0},{8,4},{1,9},{5,1},{9,5},{2,10},{6,2},{10,6},{3,11},{7,... | collective-permute-start | bytes 110600 | tf_op jit(solution)/shard_map/ppermute | solution.py:93
  135.6 5.8 %collective-permute-start.10 = (bf16[32,576]{1,0:T(8,128)(2,1)S(1)}, bf16[32,576]{1,0:T(8,128)(2,1)S(1)}, u32[]{:S(2)}, u32[]{:S(2)}) collective-permute-start(bf16[32,576]{1,0:T(8,128)(2,1)S(1)} %get-tuple-element.19), channel_id=1, source_target_pairs={{0,4},{4,8},{8,0},{1,5},{5,9},{9,1},{2,6},{6,10},{10,2},{3,7},{7,1... | collective-permute-start | bytes 110600 | tf_op jit(solution)/shard_map/ppermute | solution.py:93
  139.0 2.9 %collective-permute-start.9 = (bf16[32,576]{1,0:T(8,128)(2,1)S(1)}, bf16[32,576]{1,0:T(8,128)(2,1)S(1)}, u32[]{:S(2)}, u32[]{:S(2)}) collective-permute-start(bf16[32,576]{1,0:T(8,128)(2,1)S(1)} %get-tuple-element.21), channel_id=1, source_target_pairs={{0,12},{4,0},{8,4},{12,8},{1,13},{5,1},{9,5},{13,9},{2,14},{6,2},{... | collective-permute-start | bytes 110600 | tf_op jit(solution)/shard_map/ppermute | solution.py:93
  139.1 3.8 %collective-permute-start.8 = (bf16[32,576]{1,0:T(8,128)(2,1)S(1)}, bf16[32,576]{1,0:T(8,128)(2,1)S(1)}, u32[]{:S(2)}, u32[]{:S(2)}) collective-permute-start(bf16[32,576]{1,0:T(8,128)(2,1)S(1)} %get-tuple-element.21), channel_id=1, source_target_pairs={{0,8},{4,12},{8,0},{12,4},{1,9},{5,13},{9,1},{13,5},{2,10},{6,14},... | collective-permute-start | bytes 110600 | tf_op jit(solution)/shard_map/ppermute | solution.py:93
  140.3 4.7 %collective-permute-start.7 = (bf16[32,576]{1,0:T(8,128)(2,1)S(1)}, bf16[32,576]{1,0:T(8,128)(2,1)S(1)}, u32[]{:S(2)}, u32[]{:S(2)}) collective-permute-start(bf16[32,576]{1,0:T(8,128)(2,1)S(1)} %get-tuple-element.21), channel_id=1, source_target_pairs={{0,4},{4,8},{8,12},{12,0},{1,5},{5,9},{9,13},{13,1},{2,6},{6,10},{... | collective-permute-start | bytes 110600 | tf_op jit(solution)/shard_map/ppermute | solution.py:93
  162.0 13.2 %all-to-all-start.2 = ((bf16[16,32,576]{2,1,0:T(8,128)(2,1)}), bf16[16,32,576]{2,1,0:T(8,128)(2,1)S(1)}, u32[]{:S(2)}, u32[]{:S(2)}) async-start(bf16[16,32,576]{2,1,0:T(8,128)(2,1)} %broadcast_in_dim.81), calls=%async_computation.2 | async-start | bytes 1310720 | tf_op jit(solution)/shard_map/all_to_all | solution.py:25
  165.6 55.5 %collective-permute-start.1 = (bf16[576,256]{1,0:T(8,128)(2,1)}, bf16[576,256]{1,0:T(8,128)(2,1)}, u32[]{:S(2)}, u32[]{:S(2)}) collective-permute-start(bf16[576,256]{1,0:T(8,128)(2,1)} %constant_dynamic-slice_fusion.1), channel_id=1, source_target_pairs={{0,1},{1,0},{2,3},{3,2},{4,5},{5,4},{6,7},{7,6},{8,9},{9,8},{10,11... | collective-permute-start | bytes 884744 | tf_op jit(solution)/shard_map/ppermute | solution.py:14
  176.1 14.2 %all-to-all-start.6 = ((bf16[16,32,576]{2,1,0:T(8,128)(2,1)}), bf16[16,32,576]{2,1,0:T(8,128)(2,1)}, u32[]{:S(2)}, u32[]{:S(2)}) async-start(bf16[16,32,576]{2,1,0:T(8,128)(2,1)} %broadcast_in_dim.83), calls=%async_computation.6 | async-start | bytes 1310720 | tf_op jit(solution)/shard_map/all_to_all | solution.py:25
  191.3 13.2 %all-to-all-start.8 = ((bf16[16,32,576]{2,1,0:T(8,128)(2,1)}), bf16[16,32,576]{2,1,0:T(8,128)(2,1)S(1)}, u32[]{:S(2)}, u32[]{:S(2)}) async-start(bf16[16,32,576]{2,1,0:T(8,128)(2,1)} %broadcast_in_dim.86), calls=%async_computation.8 | async-start | bytes 1310720 | tf_op jit(solution)/shard_map/all_to_all | solution.py:25
  210.7 33.3 %collective-permute-start.13 = (bf16[256,1024]{1,0:T(8,128)(2,1)}, bf16[256,1024]{1,0:T(8,128)(2,1)}, u32[]{:S(2)}, u32[]{:S(2)}) collective-permute-start(bf16[256,1024]{1,0:T(8,128)(2,1)} %dynamic-slice_convert_fusion), channel_id=1, source_target_pairs={{0,1},{1,0},{2,3},{3,2},{4,5},{5,4},{6,7},{7,6},{8,9},{9,8},{10,11... | collective-permute-start | bytes 1572872 | tf_op jit(solution)/shard_map/ppermute | solution.py:14
  245.2 29.7 %collective-permute-start.14 = (bf16[256,1024]{1,0:T(8,128)(2,1)S(1)}, bf16[256,1024]{1,0:T(8,128)(2,1)S(1)}, u32[]{:S(2)}, u32[]{:S(2)}) collective-permute-start(bf16[256,1024]{1,0:T(8,128)(2,1)S(1)} %add_convert_fusion), channel_id=1, source_target_pairs={{0,2},{2,0},{1,3},{3,1},{4,6},{6,4},{5,7},{7,5},{8,10},{10,8},{9,1... | collective-permute-start | bytes 1572872 | tf_op jit(solution)/shard_map/ppermute | solution.py:14
  275.2 3.5 %collective-permute-start.15 = (bf16[256,1024]{1,0:T(8,128)(2,1)S(1)}, bf16[256,1024]{1,0:T(8,128)(2,1)S(1)}, u32[]{:S(2)}, u32[]{:S(2)}) collective-permute-start(bf16[256,1024]{1,0:T(8,128)(2,1)S(1)} %select_convert_fusion), channel_id=1, source_target_pairs={{0,1},{1,0},{2,3},{3,2},{4,5},{5,4},{6,7},{7,6},{8,9},{9,8},{10,11... | collective-permute-start | bytes 1572872 | tf_op jit(solution)/shard_map/ppermute | solution.py:14
  (13 other events, 164.8 us)

commit v2 on v1

v2 whole, which is shorter than its diff:
```python
import functools
import itertools
import math

import jax
import jax.numpy as jnp
from jax import lax
from jax.experimental import pallas as pl
from jax.experimental.pallas import tpu as pltpu
from jax.sharding import Mesh
from jax.sharding import PartitionSpec as P


FEAT = ("x", "y")
TOK = ("half", "core")
ALL = ("x", "y", "layer", "half", "core")
RING = 4
GRANT = 14 * 2**20


def swapped(value, axis):
    return lax.ppermute(value, axis, [(0, 1), (1, 0)])


def both(own, other, index, dim):
    first = jnp.where(index == 0, own, other)
    second = jnp.where(index == 0, other, own)
    return jnp.concatenate([first, second], axis=dim)


def turned(value, step, first):
    sizes = [lax.axis_size(name) for name in ALL]
    pairs = []
    for place in itertools.product(*(range(size) for size in sizes)):
        dim = place[-1] if first else 1 - place[-1]
        there = list(place)
        there[dim] = (there[dim] + step) % sizes[dim]
        source, sink = 0, 0
        for size, here, far in zip(sizes, place, there):
            source, sink = source * size + here, sink * size + far
        pairs.append((source, sink))
    return lax.ppermute(value, ALL, pairs)


def gathered(value, together):
    around = jnp.stack([value] + [turned(value, k, False) for k in range(1, RING)])
    if together:
        corner = around[(0,) * (around.ndim - 2)][:16, :128]
        around, _ = lax.optimization_barrier((around, swapped(corner, "core")))
    return [around] + [turned(around, j, True) for j in range(1, RING)]


def dot(left, right, left_dim, right_dim):
    return lax.dot_general(
        left,
        right,
        (((left_dim,), (right_dim,)), ((), ())),
        preferred_element_type=jnp.float32,
    )


def in_place(core, first, second, far, near, pieces, where):
    for j in range(RING):
        for k in range(RING):
            one = lax.rem(first + far * j + RING, RING)
            two = lax.rem(second + near * k + RING, RING)
            x = jnp.where(core == 0, one, two)
            y = jnp.where(core == 0, two, one)
            where(x, y, pieces[j], k)


def widths_kernel(spot_ref, *refs):
    pieces, (out_ref, moved_ref, give_ref) = refs[:RING], refs[RING:]

    def put(x, y, piece, k):
        out_ref[x, y] = piece[k]

    in_place(spot_ref[0], spot_ref[1], spot_ref[2], -1, -1, pieces, put)
    moved_ref[...] = out_ref[spot_ref[4] * 2 + spot_ref[0]]
    give_ref[...] = out_ref[spot_ref[4] * 2 + 1 - spot_ref[0]]


def widths(spot, pieces):
    _, rows, tokens = pieces[0].shape
    whole = pl.BlockSpec(memory_space=pltpu.VMEM)
    return pl.pallas_call(
        widths_kernel,
        in_specs=[pl.BlockSpec(memory_space=pltpu.SMEM)] + [whole] * RING,
        out_specs=[whole] * 3,
        out_shape=[
            jax.ShapeDtypeStruct((RING, RING, rows, tokens), jnp.bfloat16),
            jax.ShapeDtypeStruct((RING, rows, tokens), jnp.bfloat16),
            jax.ShapeDtypeStruct((RING, rows, tokens), jnp.bfloat16),
        ],
        compiler_params=pltpu.CompilerParams(vmem_limit_bytes=GRANT),
        name="widths",
    )(spot, *pieces)


def encode_kernel(spot_ref, wide_ref, bias_ref, *refs):
    weights, out_ref = refs[:4], refs[4]
    core, half = spot_ref[0], spot_ref[4]
    places = (half * 2 + core, half * 2 + 1 - core, 2 - half * 2 + core, 3 - half * 2 - core)
    pre = jnp.where(half == 0, bias_ref[0], bias_ref[1])
    for place, weight_ref in zip(places, weights):
        pre = pre + dot(wide_ref[place], weight_ref[...], 0, 0)
    out_ref[...] = jnp.maximum(pre, 0.0).astype(jnp.bfloat16)


def encode(spot, wide, bias, weights):
    cols = weights[0].shape[1]
    whole = pl.BlockSpec(memory_space=pltpu.VMEM)
    return pl.pallas_call(
        encode_kernel,
        in_specs=[pl.BlockSpec(memory_space=pltpu.SMEM)] + [whole] * 6,
        out_specs=whole,
        out_shape=jax.ShapeDtypeStruct((wide.shape[2], cols), jnp.bfloat16),
        compiler_params=pltpu.CompilerParams(vmem_limit_bytes=GRANT),
        name="encode",
    )(spot, wide, bias, *weights)


def decode_kernel(step, spot_ref, mine_ref, other_ref, weight_ref, out_ref, rows):
    core = spot_ref[0]
    far = lax.rem(spot_ref[1] + step, RING)
    nlayer, part, width = out_ref.shape[1:]

    @pl.when(core == 0)
    def _():
        @pl.when(lax.rem(far, 2) == 0)
        def _():
            rows[...] = mine_ref[far // 2]

        @pl.when(lax.rem(far, 2) == 1)
        def _():
            rows[...] = other_ref[far // 2]

    @pl.when(core == 1)
    def _():
        for block in range(RING):
            act_ref = mine_ref if block % 2 else other_ref
            place = pl.ds(pl.multiple_of(far * part, part), part)
            rows[pl.ds(block * part, part), :] = act_ref[block // 2, place, :]

    for write in range(nlayer):
        output = dot(rows[...], weight_ref[write], 1, 1).astype(jnp.bfloat16)
        out_ref[:, write] = output.reshape(RING, part, width)


def decode(step, spot, mine, other, weight, part):
    few, feats = mine.shape
    nlayer, width, _ = weight.shape
    whole = pl.BlockSpec(memory_space=pltpu.VMEM)
    return pl.pallas_call(
        functools.partial(decode_kernel, step),
        in_specs=[pl.BlockSpec(memory_space=pltpu.SMEM)] + [whole] * 3,
        out_specs=whole,
        out_shape=jax.ShapeDtypeStruct((RING, nlayer, part, width), jnp.bfloat16),
        scratch_shapes=[pltpu.VMEM((RING * part, feats), jnp.bfloat16)],
        compiler_params=pltpu.CompilerParams(vmem_limit_bytes=GRANT),
    )(spot, mine.reshape(2, few // 2, feats), other.reshape(2, few // 2, feats), weight)


def halfway_kernel(spot_ref, bias_ref, target_ref, *refs):
    taken, outs = refs[:RING], refs[RING:]
    for k in range(RING):
        place = lax.rem(spot_ref[2] + k, RING)
        total = taken[0][place].astype(jnp.float32)
        for piece in taken[1:]:
            total = total + piece[place].astype(jnp.float32)
        outs[k][...] = total.astype(outs[k].dtype)
    outs[0][spot_ref[3]] += bias_ref[...] - target_ref[...].astype(jnp.float32)


def halfway(spot, bias, target, taken):
    shape = taken[0].shape[1:]
    whole = pl.BlockSpec(memory_space=pltpu.VMEM)
    return pl.pallas_call(
        halfway_kernel,
        in_specs=[pl.BlockSpec(memory_space=pltpu.SMEM)] + [whole] * (2 + RING),
        out_specs=[whole] * RING,
        out_shape=[jax.ShapeDtypeStruct(shape, jnp.float32)]
        + [jax.ShapeDtypeStruct(shape, jnp.bfloat16)] * (RING - 1),
        compiler_params=pltpu.CompilerParams(vmem_limit_bytes=GRANT),
        name="halfway",
    )(spot, bias, target, *taken)


def back_kernel(spot_ref, *refs):
    pieces, weight_ref = refs[:RING], refs[RING]
    grad_ref, keep_ref, give_ref, total = refs[RING + 1 :]
    step = pl.program_id(0)
    core = spot_ref[0]
    _, width = grad_ref.shape[-2:]

    def put(x, y, piece, k):
        grad_ref[0, x, y] = piece[k, 0]

    in_place(core, spot_ref[1], spot_ref[2], -1, -1, pieces, put)
    term = dot(grad_ref[0].reshape(-1, width), weight_ref[0], 1, 0)

    @pl.when(step == 0)
    def _():
        total[...] = term

    @pl.when(step > 0)
    def _():
        total[...] += term

    @pl.when(step == pl.num_programs(0) - 1)
    def _():
        rows = keep_ref.shape[0] // 2
        for half in range(2):
            place = pl.ds(half * rows, rows)
            first = pl.multiple_of((half * 2 + core) * rows, rows)
            keep_ref[place, :] = total[pl.ds(first, rows), :]
            first = pl.multiple_of((half * 2 + 1 - core) * rows, rows)
            give_ref[place, :] = total[pl.ds(first, rows), :].astype(jnp.bfloat16)


def back(spot, pieces, weight):
    _, nlayer, part, width = pieces[0].shape
    feats = weight.shape[2]
    few = RING * RING * part // 2
    return pl.pallas_call(
        back_kernel,
        grid_spec=pltpu.PrefetchScalarGridSpec(
            num_scalar_prefetch=1,
            grid=(nlayer,),
            in_specs=[pl.BlockSpec((RING, 1, part, width), lambda m, _: (0, m, 0, 0))] * RING
            + [pl.BlockSpec((1, width, feats), lambda m, _: (m, 0, 0))],
            out_specs=[
                pl.BlockSpec((1, RING, RING, part, width), lambda m, _: (m, 0, 0, 0, 0)),
                pl.BlockSpec((few, feats), lambda m, _: (0, 0)),
                pl.BlockSpec((few, feats), lambda m, _: (0, 0)),
            ],
            scratch_shapes=[pltpu.VMEM((2 * few, feats), jnp.float32)],
        ),
        out_shape=[
            jax.ShapeDtypeStruct((nlayer, RING, RING, part, width), jnp.bfloat16),
            jax.ShapeDtypeStruct((few, feats), jnp.float32),
            jax.ShapeDtypeStruct((few, feats), jnp.bfloat16),
        ],
        compiler_params=pltpu.CompilerParams(vmem_limit_bytes=GRANT),
        name="back",
    )(spot, *pieces, weight)


def outer_kernel(spot_ref, mine_ref, other_ref, grad_ref, out_ref, bias_ref):
    core = spot_ref[0]
    width = grad_ref.shape[-1]
    total = dot(grad_ref[0, :, core].reshape(-1, width), mine_ref[...], 0, 0)
    total += dot(grad_ref[0, :, 1 - core].reshape(-1, width), other_ref[...], 0, 0)
    out_ref[0] = total.astype(jnp.bfloat16)

    @pl.when(pl.program_id(0) == spot_ref[3])
    def _():
        grad = grad_ref[...].reshape(-1, width).astype(jnp.float32)
        bias_ref[...] = jnp.sum(grad, axis=0, keepdims=True)


def outer(spot, mine, other, grads):
    nlayer, _, _, part, width = grads.shape
    few, feats = mine.shape
    return pl.pallas_call(
        outer_kernel,
        grid_spec=pltpu.PrefetchScalarGridSpec(
            num_scalar_prefetch=1,
            grid=(nlayer,),
            in_specs=[
                pl.BlockSpec((few, feats), lambda m, _: (0, 0)),
                pl.BlockSpec((few, feats), lambda m, _: (0, 0)),
                pl.BlockSpec((1, 2, 2, RING, part, width), lambda m, _: (m, 0, 0, 0, 0, 0)),
            ],
            out_specs=[
                pl.BlockSpec((1, width, feats), lambda m, _: (m, 0, 0)),
                pl.BlockSpec((1, width), lambda m, _: (0, 0)),
            ],
        ),
        out_shape=[
            jax.ShapeDtypeStruct((nlayer, width, feats), jnp.bfloat16),
            jax.ShapeDtypeStruct((1, width), jnp.float32),
        ],
        compiler_params=pltpu.CompilerParams(vmem_limit_bytes=GRANT),
        cost_estimate=pl.CostEstimate(
            flops=4 * nlayer * few * feats * width,
            transcendentals=0,
            bytes_accessed=2 * nlayer * feats * width,
        ),
        name="outer",
    )(spot, mine, other, grads.reshape(nlayer, 2, 2, RING, part, width))


def last_kernel(moved_ref, next_ref, mine_ref, other_ref, out_ref, bias_ref):
    mine, other = mine_ref[...], other_ref[...]
    total = dot(moved_ref[...], mine, 1, 0) + dot(next_ref[...], other, 1, 0)
    out_ref[...] = total.astype(jnp.bfloat16)
    sums = [jnp.sum(g.astype(jnp.float32), axis=0, keepdims=True) for g in (mine, other)]
    bias_ref[...] = sums[0] + sums[1]


def last(moved, moved_next, mine, other):
    width, few = moved.shape
    feats = mine.shape[1]
    cut = min(feats, 256)
    return pl.pallas_call(
        last_kernel,
        grid=(feats // cut,),
        in_specs=[
            pl.BlockSpec((width, few), lambda n: (0, 0)),
            pl.BlockSpec((width, few), lambda n: (0, 0)),
            pl.BlockSpec((few, cut), lambda n: (0, n)),
            pl.BlockSpec((few, cut), lambda n: (0, n)),
        ],
        out_specs=[
            pl.BlockSpec((width, cut), lambda n: (0, n)),
            pl.BlockSpec((1, cut), lambda n: (0, n)),
        ],
        out_shape=[
            jax.ShapeDtypeStruct((width, feats), jnp.bfloat16),
            jax.ShapeDtypeStruct((1, feats), jnp.float32),
        ],
        compiler_params=pltpu.CompilerParams(vmem_limit_bytes=GRANT),
        name="last",
    )(moved, moved_next, mine, other)


def step(captured, target, enc_weight, enc_bias, dec_weight, dec_bias):
    layer = lax.axis_index("layer")
    half = lax.axis_index("half")
    core = lax.axis_index("core")
    nlayer = dec_weight.shape[1]
    width = enc_weight.shape[1]
    feats = enc_weight.shape[2]
    rows = captured.shape[1]
    tokens = rows * lax.axis_size(TOK)
    x, y = lax.axis_index("x"), lax.axis_index("y")
    first = jnp.where(core == 0, x, y)
    second = jnp.where(core == 0, y, x)
    spot = jnp.stack([core, first, second, layer, half])
    scale = 1.0 / math.sqrt(tokens)
    encoder = enc_weight[0]
    decoder = dec_weight[0].swapaxes(1, 2)

    cols = feats // 2
    theirs = lax.dynamic_slice_in_dim(encoder, (1 - half) * cols, cols, 1)
    theirs, captured, spot = lax.optimization_barrier((theirs, captured, spot))
    crossed = swapped(theirs, "half")
    small = captured[0].T
    small = both(small, swapped(small, "half"), half, 1)
    encoder, small = lax.optimization_barrier((encoder, small))
    mine = lax.dynamic_slice_in_dim(encoder, half * cols, cols, 1)
    mine_next = swapped(mine, "core")
    pieces = gathered(small, False)
    wide, moved, give = widths(spot, pieces)
    give, crossed = lax.optimization_barrier((give, crossed))
    crossed_next = swapped(crossed, "core")
    moved_next = swapped(give.reshape(width, -1), "core")
    crossed_next, moved_next = lax.optimization_barrier((crossed_next, moved_next))
    moved = moved.reshape(width, -1)
    act = encode(
        spot,
        wide.reshape(RING, width, -1),
        enc_bias.reshape(2, 1, cols),
        (mine, mine_next, crossed, crossed_next),
    )
    act = both(act, swapped(act, "half"), half, 1)
    act_next = swapped(act, "core")

    held = decoder
    taken = [None] * RING
    for j in (2, 1, 3, 0):
        part = decode(j, spot, act, act_next, held, target.shape[1])
        taken[j] = turned(part, j, True) if j else part
    parts = halfway(spot, dec_bias, target[0], taken)
    recon = parts[0]
    for k in range(1, RING):
        recon = recon + turned(parts[k], k, False).astype(jnp.float32)
    writes = lax.broadcasted_iota(jnp.int32, (nlayer, 1, 1), 0)
    recon = jnp.where(writes >= layer, recon, 0.0)
    shared = recon.astype(jnp.bfloat16)
    for far in range(1, nlayer):
        least = min(max(k, (k + far) % nlayer) for k in range(nlayer))
        ring = [(k, (k + far) % nlayer) for k in range(nlayer)]
        taken = lax.ppermute(shared[least:], "layer", ring).astype(jnp.float32)
        recon = recon + jnp.pad(taken, ((least, 0), (0, 0), (0, 0)))
    scaled = jnp.where(writes >= layer, recon * scale, 0.0)
    pieces = gathered(scaled.astype(jnp.bfloat16), True)

    grads, keep, give = back(spot, pieces, held)
    keep = keep + swapped(give, "core").astype(jnp.float32)
    keep = lax.optimization_barrier(keep.astype(jnp.bfloat16))
    crossing = swapped(keep, "half")
    grads, _ = lax.optimization_barrier((grads, keep))
    dec_grads, dec_bias_grad = outer(spot, act, act_next, grads)
    grad_mine = keep.astype(jnp.float32) + crossing.astype(jnp.float32)
    grad_pre = jnp.where(act > 0, grad_mine, 0.0).astype(jnp.bfloat16)
    enc_grad, enc_bias_grad = last(moved, moved_next, grad_pre, swapped(grad_pre, "core"))
    return (enc_grad[None], enc_bias_grad, dec_grads.swapaxes(1, 2)[None], dec_bias_grad)


def solution(mesh):
    split = Mesh(
        mesh.devices.reshape(4, 4, mesh.shape["layer"], 2, 2),
        ("x", "y", "layer", "half", "core"),
    )
    return jax.shard_map(
        step,
        mesh=split,
        in_specs=(
            P("layer", TOK, FEAT),
            P("layer", FEAT, TOK),
            P("layer", TOK, FEAT),
            P("layer", FEAT),
            P("layer", None, FEAT, TOK),
            P("layer", TOK),
        ),
        out_specs=(
            P("layer", TOK, FEAT),
            P("layer", FEAT),
            P("layer", None, FEAT, TOK),
            P("layer", TOK),
        ),
        check_vma=False,
    )
```

time: 284 us -> 195 us (0.69)
  starting transfers between devices: 112 us -> 71.1 us
  matrix products: 36 us -> 0 us
  local copies, waits for them, and re-layouts: 30.6 us -> 1.46 us
  Pallas kernels: 0 us -> 26.1 us
  blocking collectives: 15.9 us -> 0 us
  waiting for transfers between devices: 77.2 us -> 92 us
  other arithmetic: 9.57 us -> 0.99 us
    ppermute x6 -> x21, waiting for transfers between devices: 3.48 us -> 60 us  [the longest x18 55 us: turned(): return lax.ppermute(value, ALL, pairs)]
    all_to_all x8 -> x0, starting transfers between devices: 38.3 us -> none  [the longest x4 19.8 us: on_device(): pieces = lax.all_to_all(partial, FEAT, 0, 0, tiled=True)]
    dot_general x17 -> x0, matrix products: 36 us -> none  [dot(): lax.dot_general(left, right, (((left_dim,), (right_dim,)), ((), ())), pre...]
    all_to_all x8 -> x0, waiting for transfers between devices: 28.1 us -> none  [the longest x4 17.5 us: on_device(): pieces = lax.all_to_all(partial, FEAT, 0, 0, tiled=True)]
    pallas_call x0 -> x10, Pallas kernels: none -> 26.1 us  [the longest x4 9.35 us: decode(): pl.pallas_call(functools.partial(decode_kernel, step), in_specs=[pl.Block...]
    ppermute x10, starting transfers between devices: 57.4 us -> 39.6 us  [swapped(): return lax.ppermute(value, axis, [(0, 1), (1, 0)])]
    all_to_all x1 -> x0, blocking collectives: 15.9 us -> none  [sent_to_all(): lax.all_to_all(jnp.broadcast_to(shard[None], (length, *shard.shape)), axi...]
    ppermute x6 -> x21, starting transfers between devices: 15.9 us -> 31.5 us  [the longest x18 21.4 us: turned(): return lax.ppermute(value, ALL, pairs)]
  transfers between devices with their start and end apart: 24 -> 31, of which waited for: 14 -> 23; matrix products, arithmetic and copies ran while one was open for 22% -> 0% of each run, Pallas kernels for 0% -> 4%
where the time goes in v2:
time: 195 us; the launch traced here: 193 us
  waiting for transfers between devices  92 us (47%)
  starting transfers between devices  71.1 us (36%)
  Pallas kernels  26.1 us (13%)
    ppermute x18, waiting for transfers between devices, turned(): return lax.ppermute(value, ALL, pairs)  55 us
    ppermute x10, starting transfers between devices, swapped(): return lax.ppermute(value, axis, [(0, 1), (1, 0)])  39.6 us
    ppermute x10, waiting for transfers between devices, swapped(): return lax.ppermute(value, axis, [(0, 1), (1, 0)])  31.9 us
    ppermute x18, starting transfers between devices, turned(): return lax.ppermute(value, ALL, pairs)  21.4 us
    ppermute x3, starting transfers between devices, step(): taken = lax.ppermute(shared[least:], 'layer', ring).astype(jnp.float32)  10.1 us
    pallas_call x4, Pallas kernels, decode(): pl.pallas_call(functools.partial(decode_kernel, step), in_specs=[pl.Block...  9.35 us
    pallas_call x1, Pallas kernels, back(): pl.pallas_call(back_kernel, grid_spec=pltpu.PrefetchScalarGridSpec(num_sc...  5.8 us
    pallas_call x1, Pallas kernels, outer(): pl.pallas_call(outer_kernel, grid_spec=pltpu.PrefetchScalarGridSpec(num_s...  5.16 us
  transfers between devices with their start and end apart: 31, of which 23 were waited for; matrix products, arithmetic and copies ran while one was open for 0% of the time, Pallas kernels for 4%

profile of v2, /device:TPU:1, one launch (start us, length us, event | category | flops | bytes accessed | tf_op | source)
XLA Modules:
  0.0 192.5 jit_solution(15943615353814980333)
XLA Ops:
  2.0 7.8 %collective-permute-start = (bf16[144,128]{1,0:T(8,128)(2,1)S(1)}, bf16[144,128]{1,0:T(8,128)(2,1)S(1)}, u32[]{:S(2)}, u32[]{:S(2)}) collective-permute-start(bf16[144,128]{1,0:T(8,128)(2,1)S(1)} %bitcast.64), channel_id=1, source_target_pairs={{0,2},{2,0},{1,3},{3,1},{4,6},{6,4},{5,7},{7,5},{8,10},{10,8},{9,1... | collective-permute-start | bytes 110600 | tf_op jit(solution)/shard_map/ppermute | solution.py:22
  11.2 2.6 %collective-permute-start.3 = (bf16[144,256]{1,0:T(8,128)(2,1)S(1)}, bf16[144,256]{1,0:T(8,128)(2,1)S(1)}, u32[]{:S(2)}, u32[]{:S(2)}) collective-permute-start(bf16[144,256]{1,0:T(8,128)(2,1)S(1)} %pad_maximum_fusion.3), channel_id=1, source_target_pairs={{0,48},{1,193},{2,50},{3,195},{4,52},{5,197},{6,54},{7,199},{8,56}... | collective-permute-start | bytes 221192 | tf_op jit(solution)/shard_map/ppermute | solution.py:42
  15.1 3.6 %collective-permute-done.2 = bf16[144,256]{1,0:T(8,128)(2,1)S(1)} collective-permute-done((bf16[144,256]{1,0:T(8,128)(2,1)S(1)}, bf16[144,256]{1,0:T(8,128)(2,1)S(1)}, u32[]{:S(2)}, u32[]{:S(2)}) %collective-permute-start.2) | collective-permute-done | bytes 73760 | tf_op jit(solution)/shard_map/ppermute | solution.py:42
  19.6 2.8 %collective-permute-start.6 = (bf16[4,144,256]{2,1,0:T(8,128)(2,1)S(1)}, bf16[4,144,256]{2,1,0:T(8,128)(2,1)S(1)}, u32[]{:S(2)}, u32[]{:S(2)}) collective-permute-start(bf16[4,144,256]{2,1,0:T(8,128)(2,1)S(1)} %pad_maximum_fusion.2.refs_0_), channel_id=1, source_target_pairs={{0,192},{1,49},{2,194},{3,51},{4,196},{5,53},{6,198},{7,55},{8,200... | collective-permute-start | bytes 884744 | tf_op jit(solution)/shard_map/ppermute | solution.py:42
  23.4 5.8 %collective-permute-done.6.refs_3_ = bf16[4,144,256]{2,1,0:T(8,128)(2,1)S(1)} collective-permute-done((bf16[4,144,256]{2,1,0:T(8,128)(2,1)S(1)}, bf16[4,144,256]{2,1,0:T(8,128)(2,1)S(1)}, u32[]{:S(2)}, u32[]{:S(2)}) %collective-permute-start.6) | collective-permute-done | bytes 294944 | tf_op jit(solution)/shard_map/ppermute | solution.py:42
  29.8 3.1 %collective-permute-done.4.refs_1_ = bf16[4,144,256]{2,1,0:T(8,128)(2,1)S(1)} collective-permute-done((bf16[4,144,256]{2,1,0:T(8,128)(2,1)S(1)}, bf16[4,144,256]{2,1,0:T(8,128)(2,1)S(1)}, u32[]{:S(2)}, u32[]{:S(2)}) %collective-permute-start.4) | collective-permute-done | bytes 294944 | tf_op jit(solution)/shard_map/ppermute | solution.py:42
  33.6 3.9 %collective-permute-start.8 = (bf16[576,512]{1,0:T(8,128)(2,1)S(1)}, bf16[576,512]{1,0:T(8,128)(2,1)S(1)}, u32[]{:S(2)}, u32[]{:S(2)}) collective-permute-start(bf16[576,512]{1,0:T(8,128)(2,1)S(1)} %collective-permute-done.7.refs_2_), channel_id=1, source_target_pairs={{0,1},{1,0},{2,3},{3,2},{4,5},{5,4},{6,7},{7,6},{8,9},{9,8},{10,11... | collective-permute-start | bytes 1769480 | tf_op jit(solution)/shard_map/ppermute | solution.py:22
  42.0 6.1 %collective-permute-start.11 = (bf16[256,512]{1,0:T(8,128)(2,1)S(1)}, bf16[256,512]{1,0:T(8,128)(2,1)S(1)}, u32[]{:S(2)}, u32[]{:S(2)}) collective-permute-start(bf16[256,512]{1,0:T(8,128)(2,1)S(1)} %encode.1), channel_id=1, source_target_pairs={{0,2},{2,0},{1,3},{3,1},{4,6},{6,4},{5,7},{7,5},{8,10},{10,8},{9,1... | collective-permute-start | bytes 786440 | tf_op jit(solution)/shard_map/ppermute | solution.py:22
  48.1 6.3 %collective-permute-done.11 = bf16[256,512]{1,0:T(8,128)(2,1)S(1)} collective-permute-done((bf16[256,512]{1,0:T(8,128)(2,1)S(1)}, bf16[256,512]{1,0:T(8,128)(2,1)S(1)}, u32[]{:S(2)}, u32[]{:S(2)}) %collective-permute-start.11) | collective-permute-done | bytes 262176 | tf_op jit(solution)/shard_map/ppermute | solution.py:22
  69.6 12.6 %collective-permute-done.13.refs_1_ = bf16[4,4,32,576]{3,2,1,0:T(8,128)(2,1)S(1)} collective-permute-done((bf16[4,4,32,576]{3,2,1,0:T(8,128)(2,1)S(1)}, bf16[4,4,32,576]{3,2,1,0:T(8,128)(2,1)S(1)}, u32[]{:S(2)}, u32[]{:S(2)}) %collective-permute-start.13) | collective-permute-done | bytes 589856 | tf_op jit(solution)/shard_map/ppermute | solution.py:42
  86.7 4.7 %collective-permute-done.16 = bf16[4,32,576]{2,1,0:T(8,128)(2,1)S(1)} collective-permute-done((bf16[4,32,576]{2,1,0:T(8,128)(2,1)S(1)}, bf16[4,32,576]{2,1,0:T(8,128)(2,1)S(1)}, u32[]{:S(2)}, u32[]{:S(2)}) %collective-permute-start.16) | collective-permute-done | bytes 147488 | tf_op jit(solution)/shard_map/ppermute | solution.py:42
  92.2 2.5 %collective-permute-start.21 = (bf16[3,32,576]{2,1,0:T(8,128)(2,1)S(1)}, bf16[3,32,576]{2,1,0:T(8,128)(2,1)S(1)}, u32[]{:S(2)}, u32[]{:S(2)}) collective-permute-start(bf16[3,32,576]{2,1,0:T(8,128)(2,1)S(1)} %slice.11), channel_id=1, source_target_pairs={{0,12},{4,0},{8,4},{12,8},{1,13},{5,1},{9,5},{13,9},{2,14},{6,2},{... | collective-permute-start | bytes 331784 | tf_op jit(solution)/shard_map/ppermute | solution.py:385
  94.6 5.7 %collective-permute-start.19 = (bf16[3,32,576]{2,1,0:T(8,128)(2,1)S(1)}, bf16[3,32,576]{2,1,0:T(8,128)(2,1)S(1)}, u32[]{:S(2)}, u32[]{:S(2)}) collective-permute-start(bf16[3,32,576]{2,1,0:T(8,128)(2,1)S(1)} %slice.11), channel_id=1, source_target_pairs={{0,4},{4,8},{8,12},{12,0},{1,5},{5,9},{9,13},{13,1},{2,6},{6,10},{... | collective-permute-start | bytes 331784 | tf_op jit(solution)/shard_map/ppermute | solution.py:385
  102.3 5.0 %collective-permute-done.20 = bf16[2,32,576]{2,1,0:T(8,128)(2,1)S(1)} collective-permute-done((bf16[2,32,576]{2,1,0:T(8,128)(2,1)S(1)}, bf16[2,32,576]{2,1,0:T(8,128)(2,1)S(1)}, u32[]{:S(2)}, u32[]{:S(2)}) %collective-permute-start.20) | collective-permute-done | bytes 73760 | tf_op jit(solution)/shard_map/ppermute | solution.py:385
  110.2 3.3 %collective-permute-done.24 = bf16[4,32,576]{2,1,0:T(8,128)(2,1)S(1)} collective-permute-done((bf16[4,32,576]{2,1,0:T(8,128)(2,1)S(1)}, bf16[4,32,576]{2,1,0:T(8,128)(2,1)S(1)}, u32[]{:S(2)}, u32[]{:S(2)}) %collective-permute-start.24) | collective-permute-done | bytes 147488 | tf_op jit(solution)/shard_map/ppermute | solution.py:42
  116.8 2.7 %collective-permute-start.27 = (bf16[4,4,32,576]{3,2,1,0:T(8,128)(2,1)S(1)}, bf16[4,4,32,576]{3,2,1,0:T(8,128)(2,1)S(1)}, u32[]{:S(2)}, u32[]{:S(2)}) collective-permute-start(bf16[4,4,32,576]{3,2,1,0:T(8,128)(2,1)S(1)} %pad_maximum_fusion.refs_0_), channel_id=1, source_target_pairs={{0,192},{1,49},{2,194},{3,51},{4,196},{5,53},{6,198},{7,55},{8,200... | collective-permute-start | bytes 1769480 | tf_op jit(solution)/shard_map/ppermute | solution.py:42
  122.0 6.5 %collective-permute-done.27.refs_3_ = bf16[4,4,32,576]{3,2,1,0:T(8,128)(2,1)S(1)} collective-permute-done((bf16[4,4,32,576]{3,2,1,0:T(8,128)(2,1)S(1)}, bf16[4,4,32,576]{3,2,1,0:T(8,128)(2,1)S(1)}, u32[]{:S(2)}, u32[]{:S(2)}) %collective-permute-start.27) | collective-permute-done | bytes 589856 | tf_op jit(solution)/shard_map/ppermute | solution.py:42
  130.6 7.2 %collective-permute-done.25.refs_1_ = bf16[4,4,32,576]{3,2,1,0:T(8,128)(2,1)S(1)} collective-permute-done((bf16[4,4,32,576]{3,2,1,0:T(8,128)(2,1)S(1)}, bf16[4,4,32,576]{3,2,1,0:T(8,128)(2,1)S(1)}, u32[]{:S(2)}, u32[]{:S(2)}) %collective-permute-start.25) | collective-permute-done | bytes 589856 | tf_op jit(solution)/shard_map/ppermute | solution.py:42
  137.8 5.8 %back.1 = (bf16[4,4,4,32,576]{4,3,2,1,0:T(8,128)(2,1)S(1)}, f32[256,1024]{1,0:T(8,128)S(1)}, bf16[256,1024]{1,0:T(8,128)(2,1)S(1)}) custom-call(s32[5]{0:T(128)S(1)} %stack.53.spot_ref, bf16[4,4,32,576]{3,2,1,0:T(8,128)(2,1)S(1)} %pad_maximum_fusion.refs_0_, bf16[4,4,32,576]{3,2,1,0:T(8,128)(2,1)S(1)} %collective-permute-done.25.refs_1_, ...), custom_call_target="tpu_custom_call" | custom-call | tf_op jit(solution)/shard_map/back/pallas_call | solution.py:225
  143.6 7.6 %collective-permute-start.28 = (bf16[256,1024]{1,0:T(8,128)(2,1)S(1)}, bf16[256,1024]{1,0:T(8,128)(2,1)S(1)}, u32[]{:S(2)}, u32[]{:S(2)}) collective-permute-start(bf16[256,1024]{1,0:T(8,128)(2,1)S(1)} %get-tuple-element.45), channel_id=1, source_target_pairs={{0,1},{1,0},{2,3},{3,2},{4,5},{5,4},{6,7},{7,6},{8,9},{9,8},{10,11... | collective-permute-start | bytes 1572872 | tf_op jit(solution)/shard_map/ppermute | solution.py:22
  152.9 12.0 %collective-permute-start.29 = (bf16[256,1024]{1,0:T(8,128)(2,1)S(1)}, bf16[256,1024]{1,0:T(8,128)(2,1)S(1)}, u32[]{:S(2)}, u32[]{:S(2)}) collective-permute-start(bf16[256,1024]{1,0:T(8,128)(2,1)S(1)} %add_convert_fusion), channel_id=1, source_target_pairs={{0,2},{2,0},{1,3},{3,1},{4,6},{6,4},{5,7},{7,5},{8,10},{10,8},{9,1... | collective-permute-start | bytes 1572872 | tf_op jit(solution)/shard_map/ppermute | solution.py:22
  164.9 19.1 %collective-permute-done.29 = bf16[256,1024]{1,0:T(8,128)(2,1)S(1)} collective-permute-done((bf16[256,1024]{1,0:T(8,128)(2,1)S(1)}, bf16[256,1024]{1,0:T(8,128)(2,1)S(1)}, u32[]{:S(2)}, u32[]{:S(2)}) %collective-permute-start.29) | collective-permute-done | bytes 524320 | tf_op jit(solution)/shard_map/ppermute | solution.py:22
  184.8 5.2 %outer.1 = (bf16[4,576,1024]{2,1,0:T(8,128)(2,1)}, f32[1,576]{1,0:T(1,128)}) custom-call(s32[5]{0:T(128)S(1)} %stack.53.spot_ref, bf16[256,1024]{1,0:T(8,128)(2,1)S(1)} %pad_maximum_fusion.1.mine_ref, bf16[256,1024]{1,0:T(8,128)(2,1)S(1)} %collective-permute-done.12.other_ref, bf16[4,2,2,4,32,576]{5,4,3,2,1,0:T(8,128)(2,1)S(1)} %bitcast.54), custom_call_target="tpu_custom_call" | custom-call | flops 2415919104 | bytes 4718592 | tf_op jit(solution)/shard_map/outer/pallas_call | solution.py:265
  189.9 2.6 %last.1 = (bf16[576,1024]{1,0:T(8,128)(2,1)}, f32[1,1024]{1,0:T(1,128)}) custom-call(bf16[576,256]{1,0:T(8,128)(2,1)S(1)} %bitcast.51, bf16[576,256]{1,0:T(8,128)(2,1)S(1)} %collective-permute-done.9.next_ref, bf16[256,1024]{1,0:T(8,128)(2,1)S(1)} %select_convert_fusion.mine_ref, bf16[256,1024]{1,0:T(8,128)(2,1)S(1)} %collective-permute-done.30.other_ref), custom_call_target="tpu_custom_call" | custom-call | tf_op jit(solution)/shard_map/last/pallas_call | solution.py:306
  (76 shorter events, 47.2 us)
Async XLA Ops:
  2.0 9.1 %collective-permute-start = (bf16[144,128]{1,0:T(8,128)(2,1)S(1)}, bf16[144,128]{1,0:T(8,128)(2,1)S(1)}, u32[]{:S(2)}, u32[]{:S(2)}) collective-permute-start(bf16[144,128]{1,0:T(8,128)(2,1)S(1)} %bitcast.64), channel_id=1, source_target_pairs={{0,2},{2,0},{1,3},{3,1},{4,6},{6,4},{5,7},{7,5},{8,10},{10,8},{9,1... | collective-permute-start | bytes 110600 | tf_op jit(solution)/shard_map/ppermute | solution.py:22
  9.8 23.8 %collective-permute-start.7 = (bf16[576,512]{1,0:T(8,128)(2,1)S(1)}, bf16[576,512]{1,0:T(8,128)(2,1)S(1)}, u32[]{:S(2)}, u32[]{:S(2)}) collective-permute-start(bf16[576,512]{1,0:T(8,128)(2,1)S(1)} %dynamic-slice_bitcast_fusion), channel_id=1, source_target_pairs={{0,2},{2,0},{1,3},{3,1},{4,6},{6,4},{5,7},{7,5},{8,10},{10,8},{9,1... | collective-permute-start | bytes 1769480 | tf_op jit(solution)/shard_map/ppermute | solution.py:22
  19.6 9.6 %collective-permute-start.6 = (bf16[4,144,256]{2,1,0:T(8,128)(2,1)S(1)}, bf16[4,144,256]{2,1,0:T(8,128)(2,1)S(1)}, u32[]{:S(2)}, u32[]{:S(2)}) collective-permute-start(bf16[4,144,256]{2,1,0:T(8,128)(2,1)S(1)} %pad_maximum_fusion.2.refs_0_), channel_id=1, source_target_pairs={{0,192},{1,49},{2,194},{3,51},{4,196},{5,53},{6,198},{7,55},{8,200... | collective-permute-start | bytes 884744 | tf_op jit(solution)/shard_map/ppermute | solution.py:42
  22.4 7.4 %collective-permute-start.5 = (bf16[4,144,256]{2,1,0:T(8,128)(2,1)S(1)}, bf16[4,144,256]{2,1,0:T(8,128)(2,1)S(1)}, u32[]{:S(2)}, u32[]{:S(2)}) collective-permute-start(bf16[4,144,256]{2,1,0:T(8,128)(2,1)S(1)} %pad_maximum_fusion.2.refs_0_), channel_id=1, source_target_pairs={{0,128},{1,33},{2,130},{3,35},{4,132},{5,37},{6,134},{7,39},{8,136... | collective-permute-start | bytes 884744 | tf_op jit(solution)/shard_map/ppermute | solution.py:42
  22.7 10.2 %collective-permute-start.4 = (bf16[4,144,256]{2,1,0:T(8,128)(2,1)S(1)}, bf16[4,144,256]{2,1,0:T(8,128)(2,1)S(1)}, u32[]{:S(2)}, u32[]{:S(2)}) collective-permute-start(bf16[4,144,256]{2,1,0:T(8,128)(2,1)S(1)} %pad_maximum_fusion.2.refs_0_), channel_id=1, source_target_pairs={{0,64},{1,17},{2,66},{3,19},{4,68},{5,21},{6,70},{7,23},{8,72},{9,... | collective-permute-start | bytes 884744 | tf_op jit(solution)/shard_map/ppermute | solution.py:42
  33.6 6.8 %collective-permute-start.8 = (bf16[576,512]{1,0:T(8,128)(2,1)S(1)}, bf16[576,512]{1,0:T(8,128)(2,1)S(1)}, u32[]{:S(2)}, u32[]{:S(2)}) collective-permute-start(bf16[576,512]{1,0:T(8,128)(2,1)S(1)} %collective-permute-done.7.refs_2_), channel_id=1, source_target_pairs={{0,1},{1,0},{2,3},{3,2},{4,5},{5,4},{6,7},{7,6},{8,9},{9,8},{10,11... | collective-permute-start | bytes 1769480 | tf_op jit(solution)/shard_map/ppermute | solution.py:22
  42.0 12.4 %collective-permute-start.11 = (bf16[256,512]{1,0:T(8,128)(2,1)S(1)}, bf16[256,512]{1,0:T(8,128)(2,1)S(1)}, u32[]{:S(2)}, u32[]{:S(2)}) collective-permute-start(bf16[256,512]{1,0:T(8,128)(2,1)S(1)} %encode.1), channel_id=1, source_target_pairs={{0,2},{2,0},{1,3},{3,1},{4,6},{6,4},{5,7},{7,5},{8,10},{10,8},{9,1... | collective-permute-start | bytes 786440 | tf_op jit(solution)/shard_map/ppermute | solution.py:22
  64.2 18.0 %collective-permute-start.13 = (bf16[4,4,32,576]{3,2,1,0:T(8,128)(2,1)S(1)}, bf16[4,4,32,576]{3,2,1,0:T(8,128)(2,1)S(1)}, u32[]{:S(2)}, u32[]{:S(2)}) collective-permute-start(bf16[4,4,32,576]{3,2,1,0:T(8,128)(2,1)S(1)} %shard_map.94), channel_id=1, source_target_pairs={{0,64},{1,17},{2,66},{3,19},{4,68},{5,21},{6,70},{7,23},{8,72},{9,... | collective-permute-start | bytes 1769480 | tf_op jit(solution)/shard_map/ppermute | solution.py:42
  64.3 18.0 %collective-permute-start.14 = (bf16[4,4,32,576]{3,2,1,0:T(8,128)(2,1)S(1)}, bf16[4,4,32,576]{3,2,1,0:T(8,128)(2,1)S(1)}, u32[]{:S(2)}, u32[]{:S(2)}) collective-permute-start(bf16[4,4,32,576]{3,2,1,0:T(8,128)(2,1)S(1)} %shard_map.95), channel_id=1, source_target_pairs={{0,128},{1,33},{2,130},{3,35},{4,132},{5,37},{6,134},{7,39},{8,136... | collective-permute-start | bytes 1769480 | tf_op jit(solution)/shard_map/ppermute | solution.py:42
  65.8 17.1 %collective-permute-start.15 = (bf16[4,4,32,576]{3,2,1,0:T(8,128)(2,1)S(1)}, bf16[4,4,32,576]{3,2,1,0:T(8,128)(2,1)S(1)}, u32[]{:S(2)}, u32[]{:S(2)}) collective-permute-start(bf16[4,4,32,576]{3,2,1,0:T(8,128)(2,1)S(1)} %shard_map.96), channel_id=1, source_target_pairs={{0,192},{1,49},{2,194},{3,51},{4,196},{5,53},{6,198},{7,55},{8,200... | collective-permute-start | bytes 1769480 | tf_op jit(solution)/shard_map/ppermute | solution.py:42
  83.9 7.5 %collective-permute-start.16 = (bf16[4,32,576]{2,1,0:T(8,128)(2,1)S(1)}, bf16[4,32,576]{2,1,0:T(8,128)(2,1)S(1)}, u32[]{:S(2)}, u32[]{:S(2)}) collective-permute-start(bf16[4,32,576]{2,1,0:T(8,128)(2,1)S(1)} %get-tuple-element.41), channel_id=1, source_target_pairs={{0,16},{1,65},{2,18},{3,67},{4,20},{5,69},{6,22},{7,71},{8,24},{9,... | collective-permute-start | bytes 442376 | tf_op jit(solution)/shard_map/ppermute | solution.py:42
  84.0 7.4 %collective-permute-start.17 = (bf16[4,32,576]{2,1,0:T(8,128)(2,1)S(1)}, bf16[4,32,576]{2,1,0:T(8,128)(2,1)S(1)}, u32[]{:S(2)}, u32[]{:S(2)}) collective-permute-start(bf16[4,32,576]{2,1,0:T(8,128)(2,1)S(1)} %get-tuple-element.42), channel_id=1, source_target_pairs={{0,32},{1,129},{2,34},{3,131},{4,36},{5,133},{6,38},{7,135},{8,40}... | collective-permute-start | bytes 442376 | tf_op jit(solution)/shard_map/ppermute | solution.py:42
  85.5 6.5 %collective-permute-start.18 = (bf16[4,32,576]{2,1,0:T(8,128)(2,1)S(1)}, bf16[4,32,576]{2,1,0:T(8,128)(2,1)S(1)}, u32[]{:S(2)}, u32[]{:S(2)}) collective-permute-start(bf16[4,32,576]{2,1,0:T(8,128)(2,1)S(1)} %get-tuple-element.43), channel_id=1, source_target_pairs={{0,48},{1,193},{2,50},{3,195},{4,52},{5,197},{6,54},{7,199},{8,56}... | collective-permute-start | bytes 442376 | tf_op jit(solution)/shard_map/ppermute | solution.py:42
  92.2 15.1 %collective-permute-start.21 = (bf16[3,32,576]{2,1,0:T(8,128)(2,1)S(1)}, bf16[3,32,576]{2,1,0:T(8,128)(2,1)S(1)}, u32[]{:S(2)}, u32[]{:S(2)}) collective-permute-start(bf16[3,32,576]{2,1,0:T(8,128)(2,1)S(1)} %slice.11), channel_id=1, source_target_pairs={{0,12},{4,0},{8,4},{12,8},{1,13},{5,1},{9,5},{13,9},{2,14},{6,2},{... | collective-permute-start | bytes 331784 | tf_op jit(solution)/shard_map/ppermute | solution.py:385
  94.6 12.6 %collective-permute-start.19 = (bf16[3,32,576]{2,1,0:T(8,128)(2,1)S(1)}, bf16[3,32,576]{2,1,0:T(8,128)(2,1)S(1)}, u32[]{:S(2)}, u32[]{:S(2)}) collective-permute-start(bf16[3,32,576]{2,1,0:T(8,128)(2,1)S(1)} %slice.11), channel_id=1, source_target_pairs={{0,4},{4,8},{8,12},{12,0},{1,5},{5,9},{9,13},{13,1},{2,6},{6,10},{... | collective-permute-start | bytes 331784 | tf_op jit(solution)/shard_map/ppermute | solution.py:385
  100.4 6.9 %collective-permute-start.20 = (bf16[2,32,576]{2,1,0:T(8,128)(2,1)S(1)}, bf16[2,32,576]{2,1,0:T(8,128)(2,1)S(1)}, u32[]{:S(2)}, u32[]{:S(2)}) collective-permute-start(bf16[2,32,576]{2,1,0:T(8,128)(2,1)S(1)} %slice.12), channel_id=1, source_target_pairs={{0,8},{4,12},{8,0},{12,4},{1,9},{5,13},{9,1},{13,5},{2,10},{6,14},... | collective-permute-start | bytes 221192 | tf_op jit(solution)/shard_map/ppermute | solution.py:385
  107.4 6.2 %collective-permute-start.24 = (bf16[4,32,576]{2,1,0:T(8,128)(2,1)S(1)}, bf16[4,32,576]{2,1,0:T(8,128)(2,1)S(1)}, u32[]{:S(2)}, u32[]{:S(2)}) collective-permute-start(bf16[4,32,576]{2,1,0:T(8,128)(2,1)S(1)} %select_convert_fusion.1), channel_id=1, source_target_pairs={{0,48},{1,193},{2,50},{3,195},{4,52},{5,197},{6,54},{7,199},{8,56}... | collective-permute-start | bytes 442376 | tf_op jit(solution)/shard_map/ppermute | solution.py:42
  109.6 5.8 %collective-permute-start.23 = (bf16[4,32,576]{2,1,0:T(8,128)(2,1)S(1)}, bf16[4,32,576]{2,1,0:T(8,128)(2,1)S(1)}, u32[]{:S(2)}, u32[]{:S(2)}) collective-permute-start(bf16[4,32,576]{2,1,0:T(8,128)(2,1)S(1)} %select_convert_fusion.1), channel_id=1, source_target_pairs={{0,32},{1,129},{2,34},{3,131},{4,36},{5,133},{6,38},{7,135},{8,40}... | collective-permute-start | bytes 442376 | tf_op jit(solution)/shard_map/ppermute | solution.py:42
  109.6 7.1 %collective-permute-start.22 = (bf16[4,32,576]{2,1,0:T(8,128)(2,1)S(1)}, bf16[4,32,576]{2,1,0:T(8,128)(2,1)S(1)}, u32[]{:S(2)}, u32[]{:S(2)}) collective-permute-start(bf16[4,32,576]{2,1,0:T(8,128)(2,1)S(1)} %select_convert_fusion.1), channel_id=1, source_target_pairs={{0,16},{1,65},{2,18},{3,67},{4,20},{5,69},{6,22},{7,71},{8,24},{9,... | collective-permute-start | bytes 442376 | tf_op jit(solution)/shard_map/ppermute | solution.py:42
  116.8 11.6 %collective-permute-start.27 = (bf16[4,4,32,576]{3,2,1,0:T(8,128)(2,1)S(1)}, bf16[4,4,32,576]{3,2,1,0:T(8,128)(2,1)S(1)}, u32[]{:S(2)}, u32[]{:S(2)}) collective-permute-start(bf16[4,4,32,576]{3,2,1,0:T(8,128)(2,1)S(1)} %pad_maximum_fusion.refs_0_), channel_id=1, source_target_pairs={{0,192},{1,49},{2,194},{3,51},{4,196},{5,53},{6,198},{7,55},{8,200... | collective-permute-start | bytes 1769480 | tf_op jit(solution)/shard_map/ppermute | solution.py:42
  119.6 11.0 %collective-permute-start.26 = (bf16[4,4,32,576]{3,2,1,0:T(8,128)(2,1)S(1)}, bf16[4,4,32,576]{3,2,1,0:T(8,128)(2,1)S(1)}, u32[]{:S(2)}, u32[]{:S(2)}) collective-permute-start(bf16[4,4,32,576]{3,2,1,0:T(8,128)(2,1)S(1)} %pad_maximum_fusion.refs_0_), channel_id=1, source_target_pairs={{0,128},{1,33},{2,130},{3,35},{4,132},{5,37},{6,134},{7,39},{8,136... | collective-permute-start | bytes 1769480 | tf_op jit(solution)/shard_map/ppermute | solution.py:42
  122.0 15.8 %collective-permute-start.25 = (bf16[4,4,32,576]{3,2,1,0:T(8,128)(2,1)S(1)}, bf16[4,4,32,576]{3,2,1,0:T(8,128)(2,1)S(1)}, u32[]{:S(2)}, u32[]{:S(2)}) collective-permute-start(bf16[4,4,32,576]{3,2,1,0:T(8,128)(2,1)S(1)} %pad_maximum_fusion.refs_0_), channel_id=1, source_target_pairs={{0,64},{1,17},{2,66},{3,19},{4,68},{5,21},{6,70},{7,23},{8,72},{9,... | collective-permute-start | bytes 1769480 | tf_op jit(solution)/shard_map/ppermute | solution.py:42
  143.6 9.1 %collective-permute-start.28 = (bf16[256,1024]{1,0:T(8,128)(2,1)S(1)}, bf16[256,1024]{1,0:T(8,128)(2,1)S(1)}, u32[]{:S(2)}, u32[]{:S(2)}) collective-permute-start(bf16[256,1024]{1,0:T(8,128)(2,1)S(1)} %get-tuple-element.45), channel_id=1, source_target_pairs={{0,1},{1,0},{2,3},{3,2},{4,5},{5,4},{6,7},{7,6},{8,9},{9,8},{10,11... | collective-permute-start | bytes 1572872 | tf_op jit(solution)/shard_map/ppermute | solution.py:22
  152.9 31.0 %collective-permute-start.29 = (bf16[256,1024]{1,0:T(8,128)(2,1)S(1)}, bf16[256,1024]{1,0:T(8,128)(2,1)S(1)}, u32[]{:S(2)}, u32[]{:S(2)}) collective-permute-start(bf16[256,1024]{1,0:T(8,128)(2,1)S(1)} %add_convert_fusion), channel_id=1, source_target_pairs={{0,2},{2,0},{1,3},{3,1},{4,6},{6,4},{5,7},{7,5},{8,10},{10,8},{9,1... | collective-permute-start | bytes 1572872 | tf_op jit(solution)/shard_map/ppermute | solution.py:22
  (13 other events, 101.8 us)

commit v3 on v2

--- a/solution.py
+++ b/solution.py
@@ -42,12 +42,19 @@
     return lax.ppermute(value, ALL, pairs)
 
 
-def gathered(value, together):
+def gathered(value):
     around = jnp.stack([value] + [turned(value, k, False) for k in range(1, RING)])
-    if together:
-        corner = around[(0,) * (around.ndim - 2)][:16, :128]
-        around, _ = lax.optimization_barrier((around, swapped(corner, "core")))
     return [around] + [turned(around, j, True) for j in range(1, RING)]
+
+
+def forwarded(value):
+    around = jnp.stack([value] + [turned(value, k, False) for k in range(1, RING)])
+    corner = around[(0,) * (around.ndim - 2)][:16, :128]
+    around, _ = lax.optimization_barrier((around, swapped(corner, "core")))
+    before, after = turned(around, 1, True), turned(around, RING - 1, True)
+    low = turned(before[: RING // 2], 1, True)
+    high = turned(after[RING // 2 :], RING - 1, True)
+    return around, before, (low, high), after
 
 
 def dot(left, right, left_dim, right_dim):
@@ -186,81 +193,109 @@
     )(spot, bias, target, *taken)
 
 
-def back_kernel(spot_ref, *refs):
-    pieces, weight_ref = refs[:RING], refs[RING]
-    grad_ref, keep_ref, give_ref, total = refs[RING + 1 :]
-    step = pl.program_id(0)
+def rows_of(piece, write):
+    value = piece[:, write]
+    return value.reshape(-1, value.shape[-1])
+
+
+def near_kernel(*refs):
+    pieces, weight_ref, out_ref = refs[:-2], refs[-2], refs[-1]
+    for write in range(weight_ref.shape[0]):
+        grad = jnp.concatenate([rows_of(piece, write) for piece in pieces], axis=0)
+        term = dot(grad, weight_ref[write], 1, 0)
+        if write == 0:
+            out_ref[...] = term
+        else:
+            out_ref[...] += term
+
+
+def near_rows(pieces, weight):
+    rows = len(pieces) * RING * pieces[0].shape[2]
+    whole = pl.BlockSpec(memory_space=pltpu.VMEM)
+    return pl.pallas_call(
+        near_kernel,
+        in_specs=[whole] * (len(pieces) + 1),
+        out_specs=whole,
+        out_shape=jax.ShapeDtypeStruct((rows, weight.shape[2]), jnp.float32),
+        compiler_params=pltpu.CompilerParams(vmem_limit_bytes=GRANT),
+        name="near",
+    )(*pieces, weight)
+
+
+def back_kernel(spot_ref, low_ref, high_ref, weight_ref, near_ref, keep_ref, give_ref, total):
     core = spot_ref[0]
-    _, width = grad_ref.shape[-2:]
+    part = keep_ref.shape[2]
+    for write in range(weight_ref.shape[0]):
+        grad = jnp.concatenate([rows_of(low_ref, write), rows_of(high_ref, write)], axis=0)
+        term = dot(grad, weight_ref[write], 1, 0)
+        if write == 0:
+            total[...] = term
+        else:
+            total[...] += term
+
+    def put(x, y, source, k):
+        ref, first = source
+        rows = ref[pl.ds(first + k * part, part), :]
+
+        @pl.when(lax.rem(x, 2) == core)
+        def _():
+            keep_ref[x // 2, y] = rows
+
+        @pl.when(lax.rem(x, 2) != core)
+        def _():
+            give_ref[x // 2, y] = rows.astype(jnp.bfloat16)
+
+    block = RING * part
+    sources = ((near_ref, 0), (near_ref, block), (total, 0), (near_ref, 2 * block))
+    in_place(core, spot_ref[1], spot_ref[2], -1, -1, sources, put)
+
+
+def back(spot, far, weight, near):
+    low, high = far
+    part = low.shape[2]
+    feats = weight.shape[2]
+    shape = (2, RING, part, feats)
+    whole = pl.BlockSpec(memory_space=pltpu.VMEM)
+    keep, give = pl.pallas_call(
+        back_kernel,
+        in_specs=[pl.BlockSpec(memory_space=pltpu.SMEM)] + [whole] * 4,
+        out_specs=[whole] * 2,
+        out_shape=[
+            jax.ShapeDtypeStruct(shape, jnp.float32),
+            jax.ShapeDtypeStruct(shape, jnp.bfloat16),
+        ],
+        scratch_shapes=[pltpu.VMEM((RING * part, feats), jnp.float32)],
+        compiler_params=pltpu.CompilerParams(vmem_limit_bytes=GRANT),
+        name="back",
+    )(spot, low, high, weight, near)
+    return keep.reshape(-1, feats), give.reshape(-1, feats)
+
+
+def outer_kernel(spot_ref, mine_ref, other_ref, *refs):
+    around, before, low, high, after, out_ref, bias_ref, held = refs
+    core = spot_ref[0]
+    width = held.shape[-1]
+    cut = low.shape[0]
 
     def put(x, y, piece, k):
-        grad_ref[0, x, y] = piece[k, 0]
-
-    in_place(core, spot_ref[1], spot_ref[2], -1, -1, pieces, put)
-    term = dot(grad_ref[0].reshape(-1, width), weight_ref[0], 1, 0)
-
-    @pl.when(step == 0)
-    def _():
-        total[...] = term
-
-    @pl.when(step > 0)
-    def _():
-        total[...] += term
-
-    @pl.when(step == pl.num_programs(0) - 1)
-    def _():
-        rows = keep_ref.shape[0] // 2
-        for half in range(2):
-            place = pl.ds(half * rows, rows)
-            first = pl.multiple_of((half * 2 + core) * rows, rows)
-            keep_ref[place, :] = total[pl.ds(first, rows), :]
-            first = pl.multiple_of((half * 2 + 1 - core) * rows, rows)
-            give_ref[place, :] = total[pl.ds(first, rows), :].astype(jnp.bfloat16)
-
-
-def back(spot, pieces, weight):
-    _, nlayer, part, width = pieces[0].shape
-    feats = weight.shape[2]
-    few = RING * RING * part // 2
-    return pl.pallas_call(
-        back_kernel,
-        grid_spec=pltpu.PrefetchScalarGridSpec(
-            num_scalar_prefetch=1,
-            grid=(nlayer,),
-            in_specs=[pl.BlockSpec((RING, 1, part, width), lambda m, _: (0, m, 0, 0))] * RING
-            + [pl.BlockSpec((1, width, feats), lambda m, _: (m, 0, 0))],
-            out_specs=[
-                pl.BlockSpec((1, RING, RING, part, width), lambda m, _: (m, 0, 0, 0, 0)),
-                pl.BlockSpec((few, feats), lambda m, _: (0, 0)),
-                pl.BlockSpec((few, feats), lambda m, _: (0, 0)),
-            ],
-            scratch_shapes=[pltpu.VMEM((2 * few, feats), jnp.float32)],
-        ),
-        out_shape=[
-            jax.ShapeDtypeStruct((nlayer, RING, RING, part, width), jnp.bfloat16),
-            jax.ShapeDtypeStruct((few, feats), jnp.float32),
-            jax.ShapeDtypeStruct((few, feats), jnp.bfloat16),
-        ],
-        compiler_params=pltpu.CompilerParams(vmem_limit_bytes=GRANT),
-        name="back",
-    )(spot, *pieces, weight)
-
-
-def outer_kernel(spot_ref, mine_ref, other_ref, grad_ref, out_ref, bias_ref):
-    core = spot_ref[0]
-    width = grad_ref.shape[-1]
-    total = dot(grad_ref[0, :, core].reshape(-1, width), mine_ref[...], 0, 0)
-    total += dot(grad_ref[0, :, 1 - core].reshape(-1, width), other_ref[...], 0, 0)
+        if piece is None:
+            held[x // 2, lax.rem(x, 2), y] = low[k, 0] if k < cut else high[k - cut, 0]
+        else:
+            held[x // 2, lax.rem(x, 2), y] = piece[k, 0]
+
+    in_place(core, spot_ref[1], spot_ref[2], -1, -1, (around, before, None, after), put)
+    total = dot(held[:, core].reshape(-1, width), mine_ref[...], 0, 0)
+    total += dot(held[:, 1 - core].reshape(-1, width), other_ref[...], 0, 0)
     out_ref[0] = total.astype(jnp.bfloat16)
 
     @pl.when(pl.program_id(0) == spot_ref[3])
     def _():
-        grad = grad_ref[...].reshape(-1, width).astype(jnp.float32)
+        grad = held[...].reshape(-1, width).astype(jnp.float32)
         bias_ref[...] = jnp.sum(grad, axis=0, keepdims=True)
 
 
-def outer(spot, mine, other, grads):
-    nlayer, _, _, part, width = grads.shape
+def outer(spot, mine, other, pieces):
+    _, nlayer, part, width = pieces[0].shape
     few, feats = mine.shape
     return pl.pallas_call(
         outer_kernel,
@@ -270,12 +305,16 @@
             in_specs=[
                 pl.BlockSpec((few, feats), lambda m, _: (0, 0)),
                 pl.BlockSpec((few, feats), lambda m, _: (0, 0)),
-                pl.BlockSpec((1, 2, 2, RING, part, width), lambda m, _: (m, 0, 0, 0, 0, 0)),
+            ]
+            + [
+                pl.BlockSpec((piece.shape[0], 1, part, width), lambda m, _: (0, m, 0, 0))
+                for piece in pieces
             ],
             out_specs=[
                 pl.BlockSpec((1, width, feats), lambda m, _: (m, 0, 0)),
                 pl.BlockSpec((1, width), lambda m, _: (0, 0)),
             ],
+            scratch_shapes=[pltpu.VMEM((2, 2, RING, part, width), jnp.bfloat16)],
         ),
         out_shape=[
             jax.ShapeDtypeStruct((nlayer, width, feats), jnp.bfloat16),
@@ -288,7 +327,7 @@
             bytes_accessed=2 * nlayer * feats * width,
         ),
         name="outer",
-    )(spot, mine, other, grads.reshape(nlayer, 2, 2, RING, part, width))
+    )(spot, mine, other, *pieces)
 
 
 def last_kernel(moved_ref, next_ref, mine_ref, other_ref, out_ref, bias_ref):
@@ -351,7 +390,7 @@
     encoder, small = lax.optimization_barrier((encoder, small))
     mine = lax.dynamic_slice_in_dim(encoder, half * cols, cols, 1)
     mine_next = swapped(mine, "core")
-    pieces = gathered(small, False)
+    pieces = gathered(small)
     wide, moved, give = widths(spot, pieces)
     give, crossed = lax.optimization_barrier((give, crossed))
     crossed_next = swapped(crossed, "core")
@@ -385,13 +424,14 @@
         taken = lax.ppermute(shared[least:], "layer", ring).astype(jnp.float32)
         recon = recon + jnp.pad(taken, ((least, 0), (0, 0), (0, 0)))
     scaled = jnp.where(writes >= layer, recon * scale, 0.0)
-    pieces = gathered(scaled.astype(jnp.bfloat16), True)
-
-    grads, keep, give = back(spot, pieces, held)
+    around, before, far, after = forwarded(scaled.astype(jnp.bfloat16))
+
+    near = near_rows((around, before, after), held)
+    keep, give = back(spot, far, held, near)
     keep = keep + swapped(give, "core").astype(jnp.float32)
     keep = lax.optimization_barrier(keep.astype(jnp.bfloat16))
     crossing = swapped(keep, "half")
-    grads, _ = lax.optimization_barrier((grads, keep))
+    grads, _ = lax.optimization_barrier(((around, before, *far, after), keep))
     dec_grads, dec_bias_grad = outer(spot, act, act_next, grads)
     grad_mine = keep.astype(jnp.float32) + crossing.astype(jnp.float32)
     grad_pre = jnp.where(act > 0, grad_mine, 0.0).astype(jnp.bfloat16)

time: 195 us -> 189 us (0.969); the launches traced: 193 us -> 189 us
  starting transfers between devices: 71.1 us -> 66.7 us
    ppermute x10, starting transfers between devices: 39.6 us -> 34.8 us  [swapped(): return lax.ppermute(value, axis, [(0, 1), (1, 0)])]
    ppermute x10, waiting for transfers between devices: 31.9 us -> 36.5 us  [swapped(): return lax.ppermute(value, axis, [(0, 1), (1, 0)])]
    ppermute x18 -> x19, waiting for transfers between devices: 55 us -> 52 us  [turned(): return lax.ppermute(value, ALL, pairs)]
    pallas_call x1 -> x2, Pallas kernels: 5.8 us -> 4.5 us  [the longest x1 2.59 us: near_rows(): pl.pallas_call(near_kernel, in_specs=[whole] * (len(pieces) + 1), out_spe...]
    ppermute x18 -> x19, starting transfers between devices: 21.4 us -> 21.9 us  [turned(): return lax.ppermute(value, ALL, pairs)]
  transfers between devices with their start and end apart: 31 -> 32, of which waited for: 23 -> 23; matrix products, arithmetic and copies ran while one was open for 0% -> 0% of each run, Pallas kernels for 4% -> 6%
where the time goes in v3:
time: 189 us
  waiting for transfers between devices  93.4 us (49%)
  starting transfers between devices  66.7 us (35%)
  Pallas kernels  25.6 us (14%)
    ppermute x19, waiting for transfers between devices, turned(): return lax.ppermute(value, ALL, pairs)  52 us
    ppermute x10, waiting for transfers between devices, swapped(): return lax.ppermute(value, axis, [(0, 1), (1, 0)])  36.5 us
    ppermute x10, starting transfers between devices, swapped(): return lax.ppermute(value, axis, [(0, 1), (1, 0)])  34.8 us
    ppermute x19, starting transfers between devices, turned(): return lax.ppermute(value, ALL, pairs)  21.9 us
    ppermute x3, starting transfers between devices, step(): taken = lax.ppermute(shared[least:], 'layer', ring).astype(jnp.float32)  10.1 us
    pallas_call x4, Pallas kernels, decode(): pl.pallas_call(functools.partial(decode_kernel, step), in_specs=[pl.Block...  9.35 us
    pallas_call x1, Pallas kernels, outer(): pl.pallas_call(outer_kernel, grid_spec=pltpu.PrefetchScalarGridSpec(num_s...  5.91 us
    ppermute x3, waiting for transfers between devices, step(): taken = lax.ppermute(shared[least:], 'layer', ring).astype(jnp.float32)  5 us
  transfers between devices with their start and end apart: 32, of which 23 were waited for; matrix products, arithmetic and copies ran while one was open for 0% of the time, Pallas kernels for 6%

profile of v3, /device:TPU:1, one launch (start us, length us, event | category | flops | bytes accessed | tf_op | source)
XLA Modules:
  0.0 189.1 jit_solution(8882015161402980669)
XLA Ops:
  2.0 7.8 %collective-permute-start = (bf16[144,128]{1,0:T(8,128)(2,1)S(1)}, bf16[144,128]{1,0:T(8,128)(2,1)S(1)}, u32[]{:S(2)}, u32[]{:S(2)}) collective-permute-start(bf16[144,128]{1,0:T(8,128)(2,1)S(1)} %bitcast.69), channel_id=1, source_target_pairs={{0,2},{2,0},{1,3},{3,1},{4,6},{6,4},{5,7},{7,5},{8,10},{10,8},{9,1... | collective-permute-start | bytes 110600 | tf_op jit(solution)/shard_map/ppermute | solution.py:22
  11.2 2.6 %collective-permute-start.3 = (bf16[144,256]{1,0:T(8,128)(2,1)S(1)}, bf16[144,256]{1,0:T(8,128)(2,1)S(1)}, u32[]{:S(2)}, u32[]{:S(2)}) collective-permute-start(bf16[144,256]{1,0:T(8,128)(2,1)S(1)} %pad_maximum_fusion.3), channel_id=1, source_target_pairs={{0,48},{1,193},{2,50},{3,195},{4,52},{5,197},{6,54},{7,199},{8,56}... | collective-permute-start | bytes 221192 | tf_op jit(solution)/shard_map/ppermute | solution.py:42
  15.1 3.6 %collective-permute-done.2 = bf16[144,256]{1,0:T(8,128)(2,1)S(1)} collective-permute-done((bf16[144,256]{1,0:T(8,128)(2,1)S(1)}, bf16[144,256]{1,0:T(8,128)(2,1)S(1)}, u32[]{:S(2)}, u32[]{:S(2)}) %collective-permute-start.2) | collective-permute-done | bytes 73760 | tf_op jit(solution)/shard_map/ppermute | solution.py:42
  19.6 2.8 %collective-permute-start.6 = (bf16[4,144,256]{2,1,0:T(8,128)(2,1)S(1)}, bf16[4,144,256]{2,1,0:T(8,128)(2,1)S(1)}, u32[]{:S(2)}, u32[]{:S(2)}) collective-permute-start(bf16[4,144,256]{2,1,0:T(8,128)(2,1)S(1)} %pad_maximum_fusion.2.refs_0_), channel_id=1, source_target_pairs={{0,192},{1,49},{2,194},{3,51},{4,196},{5,53},{6,198},{7,55},{8,200... | collective-permute-start | bytes 884744 | tf_op jit(solution)/shard_map/ppermute | solution.py:42
  23.4 5.8 %collective-permute-done.6.refs_3_ = bf16[4,144,256]{2,1,0:T(8,128)(2,1)S(1)} collective-permute-done((bf16[4,144,256]{2,1,0:T(8,128)(2,1)S(1)}, bf16[4,144,256]{2,1,0:T(8,128)(2,1)S(1)}, u32[]{:S(2)}, u32[]{:S(2)}) %collective-permute-start.6) | collective-permute-done | bytes 294944 | tf_op jit(solution)/shard_map/ppermute | solution.py:42
  29.8 3.1 %collective-permute-done.4.refs_1_ = bf16[4,144,256]{2,1,0:T(8,128)(2,1)S(1)} collective-permute-done((bf16[4,144,256]{2,1,0:T(8,128)(2,1)S(1)}, bf16[4,144,256]{2,1,0:T(8,128)(2,1)S(1)}, u32[]{:S(2)}, u32[]{:S(2)}) %collective-permute-start.4) | collective-permute-done | bytes 294944 | tf_op jit(solution)/shard_map/ppermute | solution.py:42
  33.6 3.9 %collective-permute-start.8 = (bf16[576,512]{1,0:T(8,128)(2,1)S(1)}, bf16[576,512]{1,0:T(8,128)(2,1)S(1)}, u32[]{:S(2)}, u32[]{:S(2)}) collective-permute-start(bf16[576,512]{1,0:T(8,128)(2,1)S(1)} %collective-permute-done.7.refs_2_), channel_id=1, source_target_pairs={{0,1},{1,0},{2,3},{3,2},{4,5},{5,4},{6,7},{7,6},{8,9},{9,8},{10,11... | collective-permute-start | bytes 1769480 | tf_op jit(solution)/shard_map/ppermute | solution.py:22
  42.0 6.1 %collective-permute-start.11 = (bf16[256,512]{1,0:T(8,128)(2,1)S(1)}, bf16[256,512]{1,0:T(8,128)(2,1)S(1)}, u32[]{:S(2)}, u32[]{:S(2)}) collective-permute-start(bf16[256,512]{1,0:T(8,128)(2,1)S(1)} %encode.1), channel_id=1, source_target_pairs={{0,2},{2,0},{1,3},{3,1},{4,6},{6,4},{5,7},{7,5},{8,10},{10,8},{9,1... | collective-permute-start | bytes 786440 | tf_op jit(solution)/shard_map/ppermute | solution.py:22
  48.1 6.3 %collective-permute-done.11 = bf16[256,512]{1,0:T(8,128)(2,1)S(1)} collective-permute-done((bf16[256,512]{1,0:T(8,128)(2,1)S(1)}, bf16[256,512]{1,0:T(8,128)(2,1)S(1)}, u32[]{:S(2)}, u32[]{:S(2)}) %collective-permute-start.11) | collective-permute-done | bytes 262176 | tf_op jit(solution)/shard_map/ppermute | solution.py:22
  69.6 12.6 %collective-permute-done.13.refs_1_ = bf16[4,4,32,576]{3,2,1,0:T(8,128)(2,1)S(1)} collective-permute-done((bf16[4,4,32,576]{3,2,1,0:T(8,128)(2,1)S(1)}, bf16[4,4,32,576]{3,2,1,0:T(8,128)(2,1)S(1)}, u32[]{:S(2)}, u32[]{:S(2)}) %collective-permute-start.13) | collective-permute-done | bytes 589856 | tf_op jit(solution)/shard_map/ppermute | solution.py:42
  86.7 4.7 %collective-permute-done.16 = bf16[4,32,576]{2,1,0:T(8,128)(2,1)S(1)} collective-permute-done((bf16[4,32,576]{2,1,0:T(8,128)(2,1)S(1)}, bf16[4,32,576]{2,1,0:T(8,128)(2,1)S(1)}, u32[]{:S(2)}, u32[]{:S(2)}) %collective-permute-start.16) | collective-permute-done | bytes 147488 | tf_op jit(solution)/shard_map/ppermute | solution.py:42
  92.2 2.5 %collective-permute-start.21 = (bf16[3,32,576]{2,1,0:T(8,128)(2,1)S(1)}, bf16[3,32,576]{2,1,0:T(8,128)(2,1)S(1)}, u32[]{:S(2)}, u32[]{:S(2)}) collective-permute-start(bf16[3,32,576]{2,1,0:T(8,128)(2,1)S(1)} %slice.19), channel_id=1, source_target_pairs={{0,12},{4,0},{8,4},{12,8},{1,13},{5,1},{9,5},{13,9},{2,14},{6,2},{... | collective-permute-start | bytes 331784 | tf_op jit(solution)/shard_map/ppermute | solution.py:424
  94.6 5.7 %collective-permute-start.19 = (bf16[3,32,576]{2,1,0:T(8,128)(2,1)S(1)}, bf16[3,32,576]{2,1,0:T(8,128)(2,1)S(1)}, u32[]{:S(2)}, u32[]{:S(2)}) collective-permute-start(bf16[3,32,576]{2,1,0:T(8,128)(2,1)S(1)} %slice.19), channel_id=1, source_target_pairs={{0,4},{4,8},{8,12},{12,0},{1,5},{5,9},{9,13},{13,1},{2,6},{6,10},{... | collective-permute-start | bytes 331784 | tf_op jit(solution)/shard_map/ppermute | solution.py:424
  102.3 5.0 %collective-permute-done.20 = bf16[2,32,576]{2,1,0:T(8,128)(2,1)S(1)} collective-permute-done((bf16[2,32,576]{2,1,0:T(8,128)(2,1)S(1)}, bf16[2,32,576]{2,1,0:T(8,128)(2,1)S(1)}, u32[]{:S(2)}, u32[]{:S(2)}) %collective-permute-start.20) | collective-permute-done | bytes 73760 | tf_op jit(solution)/shard_map/ppermute | solution.py:424
  110.3 3.3 %collective-permute-done.24 = bf16[4,32,576]{2,1,0:T(8,128)(2,1)S(1)} collective-permute-done((bf16[4,32,576]{2,1,0:T(8,128)(2,1)S(1)}, bf16[4,32,576]{2,1,0:T(8,128)(2,1)S(1)}, u32[]{:S(2)}, u32[]{:S(2)}) %collective-permute-start.24) | collective-permute-done | bytes 147488 | tf_op jit(solution)/shard_map/ppermute | solution.py:42
  116.9 3.0 %collective-permute-start.27 = (bf16[4,4,32,576]{3,2,1,0:T(8,128)(2,1)S(1)}, bf16[4,4,32,576]{3,2,1,0:T(8,128)(2,1)S(1)}, u32[]{:S(2)}, u32[]{:S(2)}) collective-permute-start(bf16[4,4,32,576]{3,2,1,0:T(8,128)(2,1)S(1)} %pad_maximum_fusion.refs_0_), channel_id=1, source_target_pairs={{0,192},{1,49},{2,194},{3,51},{4,196},{5,53},{6,198},{7,55},{8,200... | collective-permute-start | bytes 1769480 | tf_op jit(solution)/shard_map/ppermute | solution.py:42
  120.3 8.2 %collective-permute-done.27.refs_2_.refs_4_ = bf16[4,4,32,576]{3,2,1,0:T(8,128)(2,1)S(1)} collective-permute-done((bf16[4,4,32,576]{3,2,1,0:T(8,128)(2,1)S(1)}, bf16[4,4,32,576]{3,2,1,0:T(8,128)(2,1)S(1)}, u32[]{:S(2)}, u32[]{:S(2)}) %collective-permute-start.27) | collective-permute-done | bytes 589856 | tf_op jit(solution)/shard_map/ppermute | solution.py:42
  130.8 2.6 %near.1.near_ref = f32[384,1024]{1,0:T(8,128)S(1)} custom-call(bf16[4,4,32,576]{3,2,1,0:T(8,128)(2,1)S(1)} %pad_maximum_fusion.refs_0_, bf16[4,4,32,576]{3,2,1,0:T(8,128)(2,1)S(1)} %collective-permute-done.25.refs_1_, bf16[4,4,32,576]{3,2,1,0:T(8,128)(2,1)S(1)} %collective-permute-done.27.refs_2_.refs_4_, bf16[4,576,1024]{2,1,0:T(8,128)(2,1)S(1)} %bitcast.45), custom_call_target="tpu_custom_call" | custom-call | tf_op jit(solution)/shard_map/near/pallas_call | solution.py:215
  134.8 3.1 %collective-permute-done.26.low_ref.refs_2_ = bf16[2,4,32,576]{3,2,1,0:T(8,128)(2,1)S(1)} collective-permute-done((bf16[2,4,32,576]{3,2,1,0:T(8,128)(2,1)S(1)}, bf16[2,4,32,576]{3,2,1,0:T(8,128)(2,1)S(1)}, u32[]{:S(2)}, u32[]{:S(2)}) %collective-permute-start.26) | collective-permute-done | bytes 294944 | tf_op jit(solution)/shard_map/ppermute | solution.py:42
  139.9 9.0 %collective-permute-start.29 = (bf16[256,1024]{1,0:T(8,128)(2,1)S(1)}, bf16[256,1024]{1,0:T(8,128)(2,1)S(1)}, u32[]{:S(2)}, u32[]{:S(2)}) collective-permute-start(bf16[256,1024]{1,0:T(8,128)(2,1)S(1)} %bitcast.59), channel_id=1, source_target_pairs={{0,1},{1,0},{2,3},{3,2},{4,5},{5,4},{6,7},{7,6},{8,9},{9,8},{10,11... | collective-permute-start | bytes 1572872 | tf_op jit(solution)/shard_map/ppermute | solution.py:22
  150.6 4.9 %collective-permute-start.30 = (bf16[256,1024]{1,0:T(8,128)(2,1)S(1)}, bf16[256,1024]{1,0:T(8,128)(2,1)S(1)}, u32[]{:S(2)}, u32[]{:S(2)}) collective-permute-start(bf16[256,1024]{1,0:T(8,128)(2,1)S(1)} %fusion), channel_id=1, source_target_pairs={{0,2},{2,0},{1,3},{3,1},{4,6},{6,4},{5,7},{7,5},{8,10},{10,8},{9,1... | collective-permute-start | bytes 1572872 | tf_op jit(solution)/shard_map/ppermute | solution.py:22
  155.4 23.6 %collective-permute-done.30 = bf16[256,1024]{1,0:T(8,128)(2,1)S(1)} collective-permute-done((bf16[256,1024]{1,0:T(8,128)(2,1)S(1)}, bf16[256,1024]{1,0:T(8,128)(2,1)S(1)}, u32[]{:S(2)}, u32[]{:S(2)}) %collective-permute-start.30) | collective-permute-done | bytes 524320 | tf_op jit(solution)/shard_map/ppermute | solution.py:22
  180.6 5.9 %outer.1 = (bf16[4,576,1024]{2,1,0:T(8,128)(2,1)}, f32[1,576]{1,0:T(1,128)}) custom-call(s32[5]{0:T(128)S(1)} %stack.53.spot_ref, bf16[256,1024]{1,0:T(8,128)(2,1)S(1)} %pad_maximum_fusion.1.mine_ref, bf16[256,1024]{1,0:T(8,128)(2,1)S(1)} %collective-permute-done.12.other_ref, bf16[4,4,32,576]{3,2,1,0:T(8,128)(2,1)S(1)} %pad_maximum_fusion.refs_0_, ...), custom_call_target="tpu_custom_call" | custom-call | flops 2415919104 | bytes 4718592 | tf_op jit(solution)/shard_map/outer/pallas_call | solution.py:300
  186.6 2.6 %last.1 = (bf16[576,1024]{1,0:T(8,128)(2,1)}, f32[1,1024]{1,0:T(1,128)}) custom-call(bf16[576,256]{1,0:T(8,128)(2,1)S(1)} %bitcast.56, bf16[576,256]{1,0:T(8,128)(2,1)S(1)} %collective-permute-done.9.next_ref, bf16[256,1024]{1,0:T(8,128)(2,1)S(1)} %select_convert_fusion.mine_ref, bf16[256,1024]{1,0:T(8,128)(2,1)S(1)} %collective-permute-done.31.other_ref), custom_call_target="tpu_custom_call" | custom-call | tf_op jit(solution)/shard_map/last/pallas_call | solution.py:345
  (81 shorter events, 49.5 us)
Async XLA Ops:
  2.0 9.1 %collective-permute-start = (bf16[144,128]{1,0:T(8,128)(2,1)S(1)}, bf16[144,128]{1,0:T(8,128)(2,1)S(1)}, u32[]{:S(2)}, u32[]{:S(2)}) collective-permute-start(bf16[144,128]{1,0:T(8,128)(2,1)S(1)} %bitcast.69), channel_id=1, source_target_pairs={{0,2},{2,0},{1,3},{3,1},{4,6},{6,4},{5,7},{7,5},{8,10},{10,8},{9,1... | collective-permute-start | bytes 110600 | tf_op jit(solution)/shard_map/ppermute | solution.py:22
  9.8 23.8 %collective-permute-start.7 = (bf16[576,512]{1,0:T(8,128)(2,1)S(1)}, bf16[576,512]{1,0:T(8,128)(2,1)S(1)}, u32[]{:S(2)}, u32[]{:S(2)}) collective-permute-start(bf16[576,512]{1,0:T(8,128)(2,1)S(1)} %dynamic-slice_bitcast_fusion), channel_id=1, source_target_pairs={{0,2},{2,0},{1,3},{3,1},{4,6},{6,4},{5,7},{7,5},{8,10},{10,8},{9,1... | collective-permute-start | bytes 1769480 | tf_op jit(solution)/shard_map/ppermute | solution.py:22
  19.6 9.6 %collective-permute-start.6 = (bf16[4,144,256]{2,1,0:T(8,128)(2,1)S(1)}, bf16[4,144,256]{2,1,0:T(8,128)(2,1)S(1)}, u32[]{:S(2)}, u32[]{:S(2)}) collective-permute-start(bf16[4,144,256]{2,1,0:T(8,128)(2,1)S(1)} %pad_maximum_fusion.2.refs_0_), channel_id=1, source_target_pairs={{0,192},{1,49},{2,194},{3,51},{4,196},{5,53},{6,198},{7,55},{8,200... | collective-permute-start | bytes 884744 | tf_op jit(solution)/shard_map/ppermute | solution.py:42
  22.4 7.4 %collective-permute-start.5 = (bf16[4,144,256]{2,1,0:T(8,128)(2,1)S(1)}, bf16[4,144,256]{2,1,0:T(8,128)(2,1)S(1)}, u32[]{:S(2)}, u32[]{:S(2)}) collective-permute-start(bf16[4,144,256]{2,1,0:T(8,128)(2,1)S(1)} %pad_maximum_fusion.2.refs_0_), channel_id=1, source_target_pairs={{0,128},{1,33},{2,130},{3,35},{4,132},{5,37},{6,134},{7,39},{8,136... | collective-permute-start | bytes 884744 | tf_op jit(solution)/shard_map/ppermute | solution.py:42
  22.7 10.2 %collective-permute-start.4 = (bf16[4,144,256]{2,1,0:T(8,128)(2,1)S(1)}, bf16[4,144,256]{2,1,0:T(8,128)(2,1)S(1)}, u32[]{:S(2)}, u32[]{:S(2)}) collective-permute-start(bf16[4,144,256]{2,1,0:T(8,128)(2,1)S(1)} %pad_maximum_fusion.2.refs_0_), channel_id=1, source_target_pairs={{0,64},{1,17},{2,66},{3,19},{4,68},{5,21},{6,70},{7,23},{8,72},{9,... | collective-permute-start | bytes 884744 | tf_op jit(solution)/shard_map/ppermute | solution.py:42
  33.6 6.8 %collective-permute-start.8 = (bf16[576,512]{1,0:T(8,128)(2,1)S(1)}, bf16[576,512]{1,0:T(8,128)(2,1)S(1)}, u32[]{:S(2)}, u32[]{:S(2)}) collective-permute-start(bf16[576,512]{1,0:T(8,128)(2,1)S(1)} %collective-permute-done.7.refs_2_), channel_id=1, source_target_pairs={{0,1},{1,0},{2,3},{3,2},{4,5},{5,4},{6,7},{7,6},{8,9},{9,8},{10,11... | collective-permute-start | bytes 1769480 | tf_op jit(solution)/shard_map/ppermute | solution.py:22
  42.0 12.4 %collective-permute-start.11 = (bf16[256,512]{1,0:T(8,128)(2,1)S(1)}, bf16[256,512]{1,0:T(8,128)(2,1)S(1)}, u32[]{:S(2)}, u32[]{:S(2)}) collective-permute-start(bf16[256,512]{1,0:T(8,128)(2,1)S(1)} %encode.1), channel_id=1, source_target_pairs={{0,2},{2,0},{1,3},{3,1},{4,6},{6,4},{5,7},{7,5},{8,10},{10,8},{9,1... | collective-permute-start | bytes 786440 | tf_op jit(solution)/shard_map/ppermute | solution.py:22
  64.2 18.0 %collective-permute-start.13 = (bf16[4,4,32,576]{3,2,1,0:T(8,128)(2,1)S(1)}, bf16[4,4,32,576]{3,2,1,0:T(8,128)(2,1)S(1)}, u32[]{:S(2)}, u32[]{:S(2)}) collective-permute-start(bf16[4,4,32,576]{3,2,1,0:T(8,128)(2,1)S(1)} %shard_map.94), channel_id=1, source_target_pairs={{0,64},{1,17},{2,66},{3,19},{4,68},{5,21},{6,70},{7,23},{8,72},{9,... | collective-permute-start | bytes 1769480 | tf_op jit(solution)/shard_map/ppermute | solution.py:42
  64.3 18.0 %collective-permute-start.14 = (bf16[4,4,32,576]{3,2,1,0:T(8,128)(2,1)S(1)}, bf16[4,4,32,576]{3,2,1,0:T(8,128)(2,1)S(1)}, u32[]{:S(2)}, u32[]{:S(2)}) collective-permute-start(bf16[4,4,32,576]{3,2,1,0:T(8,128)(2,1)S(1)} %shard_map.95), channel_id=1, source_target_pairs={{0,128},{1,33},{2,130},{3,35},{4,132},{5,37},{6,134},{7,39},{8,136... | collective-permute-start | bytes 1769480 | tf_op jit(solution)/shard_map/ppermute | solution.py:42
  65.8 17.1 %collective-permute-start.15 = (bf16[4,4,32,576]{3,2,1,0:T(8,128)(2,1)S(1)}, bf16[4,4,32,576]{3,2,1,0:T(8,128)(2,1)S(1)}, u32[]{:S(2)}, u32[]{:S(2)}) collective-permute-start(bf16[4,4,32,576]{3,2,1,0:T(8,128)(2,1)S(1)} %shard_map.96), channel_id=1, source_target_pairs={{0,192},{1,49},{2,194},{3,51},{4,196},{5,53},{6,198},{7,55},{8,200... | collective-permute-start | bytes 1769480 | tf_op jit(solution)/shard_map/ppermute | solution.py:42
  83.9 7.5 %collective-permute-start.16 = (bf16[4,32,576]{2,1,0:T(8,128)(2,1)S(1)}, bf16[4,32,576]{2,1,0:T(8,128)(2,1)S(1)}, u32[]{:S(2)}, u32[]{:S(2)}) collective-permute-start(bf16[4,32,576]{2,1,0:T(8,128)(2,1)S(1)} %get-tuple-element.44), channel_id=1, source_target_pairs={{0,16},{1,65},{2,18},{3,67},{4,20},{5,69},{6,22},{7,71},{8,24},{9,... | collective-permute-start | bytes 442376 | tf_op jit(solution)/shard_map/ppermute | solution.py:42
  84.0 7.4 %collective-permute-start.17 = (bf16[4,32,576]{2,1,0:T(8,128)(2,1)S(1)}, bf16[4,32,576]{2,1,0:T(8,128)(2,1)S(1)}, u32[]{:S(2)}, u32[]{:S(2)}) collective-permute-start(bf16[4,32,576]{2,1,0:T(8,128)(2,1)S(1)} %get-tuple-element.45), channel_id=1, source_target_pairs={{0,32},{1,129},{2,34},{3,131},{4,36},{5,133},{6,38},{7,135},{8,40}... | collective-permute-start | bytes 442376 | tf_op jit(solution)/shard_map/ppermute | solution.py:42
  85.5 6.5 %collective-permute-start.18 = (bf16[4,32,576]{2,1,0:T(8,128)(2,1)S(1)}, bf16[4,32,576]{2,1,0:T(8,128)(2,1)S(1)}, u32[]{:S(2)}, u32[]{:S(2)}) collective-permute-start(bf16[4,32,576]{2,1,0:T(8,128)(2,1)S(1)} %get-tuple-element.46), channel_id=1, source_target_pairs={{0,48},{1,193},{2,50},{3,195},{4,52},{5,197},{6,54},{7,199},{8,56}... | collective-permute-start | bytes 442376 | tf_op jit(solution)/shard_map/ppermute | solution.py:42
  92.2 15.1 %collective-permute-start.21 = (bf16[3,32,576]{2,1,0:T(8,128)(2,1)S(1)}, bf16[3,32,576]{2,1,0:T(8,128)(2,1)S(1)}, u32[]{:S(2)}, u32[]{:S(2)}) collective-permute-start(bf16[3,32,576]{2,1,0:T(8,128)(2,1)S(1)} %slice.19), channel_id=1, source_target_pairs={{0,12},{4,0},{8,4},{12,8},{1,13},{5,1},{9,5},{13,9},{2,14},{6,2},{... | collective-permute-start | bytes 331784 | tf_op jit(solution)/shard_map/ppermute | solution.py:424
  94.6 12.6 %collective-permute-start.19 = (bf16[3,32,576]{2,1,0:T(8,128)(2,1)S(1)}, bf16[3,32,576]{2,1,0:T(8,128)(2,1)S(1)}, u32[]{:S(2)}, u32[]{:S(2)}) collective-permute-start(bf16[3,32,576]{2,1,0:T(8,128)(2,1)S(1)} %slice.19), channel_id=1, source_target_pairs={{0,4},{4,8},{8,12},{12,0},{1,5},{5,9},{9,13},{13,1},{2,6},{6,10},{... | collective-permute-start | bytes 331784 | tf_op jit(solution)/shard_map/ppermute | solution.py:424
  100.4 6.9 %collective-permute-start.20 = (bf16[2,32,576]{2,1,0:T(8,128)(2,1)S(1)}, bf16[2,32,576]{2,1,0:T(8,128)(2,1)S(1)}, u32[]{:S(2)}, u32[]{:S(2)}) collective-permute-start(bf16[2,32,576]{2,1,0:T(8,128)(2,1)S(1)} %slice.20), channel_id=1, source_target_pairs={{0,8},{4,12},{8,0},{12,4},{1,9},{5,13},{9,1},{13,5},{2,10},{6,14},... | collective-permute-start | bytes 221192 | tf_op jit(solution)/shard_map/ppermute | solution.py:424
  109.6 7.1 %collective-permute-start.22 = (bf16[4,32,576]{2,1,0:T(8,128)(2,1)S(1)}, bf16[4,32,576]{2,1,0:T(8,128)(2,1)S(1)}, u32[]{:S(2)}, u32[]{:S(2)}) collective-permute-start(bf16[4,32,576]{2,1,0:T(8,128)(2,1)S(1)} %select_convert_fusion.1), channel_id=1, source_target_pairs={{0,16},{1,65},{2,18},{3,67},{4,20},{5,69},{6,22},{7,71},{8,24},{9,... | collective-permute-start | bytes 442376 | tf_op jit(solution)/shard_map/ppermute | solution.py:42
  116.9 11.6 %collective-permute-start.27 = (bf16[4,4,32,576]{3,2,1,0:T(8,128)(2,1)S(1)}, bf16[4,4,32,576]{3,2,1,0:T(8,128)(2,1)S(1)}, u32[]{:S(2)}, u32[]{:S(2)}) collective-permute-start(bf16[4,4,32,576]{3,2,1,0:T(8,128)(2,1)S(1)} %pad_maximum_fusion.refs_0_), channel_id=1, source_target_pairs={{0,192},{1,49},{2,194},{3,51},{4,196},{5,53},{6,198},{7,55},{8,200... | collective-permute-start | bytes 1769480 | tf_op jit(solution)/shard_map/ppermute | solution.py:42
  119.9 10.8 %collective-permute-start.25 = (bf16[4,4,32,576]{3,2,1,0:T(8,128)(2,1)S(1)}, bf16[4,4,32,576]{3,2,1,0:T(8,128)(2,1)S(1)}, u32[]{:S(2)}, u32[]{:S(2)}) collective-permute-start(bf16[4,4,32,576]{3,2,1,0:T(8,128)(2,1)S(1)} %pad_maximum_fusion.refs_0_), channel_id=1, source_target_pairs={{0,64},{1,17},{2,66},{3,19},{4,68},{5,21},{6,70},{7,23},{8,72},{9,... | collective-permute-start | bytes 1769480 | tf_op jit(solution)/shard_map/ppermute | solution.py:42
  128.5 6.3 %collective-permute-start.28 = (bf16[2,4,32,576]{3,2,1,0:T(8,128)(2,1)S(1)}, bf16[2,4,32,576]{3,2,1,0:T(8,128)(2,1)S(1)}, u32[]{:S(2)}, u32[]{:S(2)}) collective-permute-start(bf16[2,4,32,576]{3,2,1,0:T(8,128)(2,1)S(1)} %slice.22), channel_id=1, source_target_pairs={{0,192},{1,49},{2,194},{3,51},{4,196},{5,53},{6,198},{7,55},{8,200... | collective-permute-start | bytes 884744 | tf_op jit(solution)/shard_map/ppermute | solution.py:42
  130.7 7.3 %collective-permute-start.26 = (bf16[2,4,32,576]{3,2,1,0:T(8,128)(2,1)S(1)}, bf16[2,4,32,576]{3,2,1,0:T(8,128)(2,1)S(1)}, u32[]{:S(2)}, u32[]{:S(2)}) collective-permute-start(bf16[2,4,32,576]{3,2,1,0:T(8,128)(2,1)S(1)} %slice.21), channel_id=1, source_target_pairs={{0,64},{1,17},{2,66},{3,19},{4,68},{5,21},{6,70},{7,23},{8,72},{9,... | collective-permute-start | bytes 884744 | tf_op jit(solution)/shard_map/ppermute | solution.py:42
  139.9 10.5 %collective-permute-start.29 = (bf16[256,1024]{1,0:T(8,128)(2,1)S(1)}, bf16[256,1024]{1,0:T(8,128)(2,1)S(1)}, u32[]{:S(2)}, u32[]{:S(2)}) collective-permute-start(bf16[256,1024]{1,0:T(8,128)(2,1)S(1)} %bitcast.59), channel_id=1, source_target_pairs={{0,1},{1,0},{2,3},{3,2},{4,5},{5,4},{6,7},{7,6},{8,9},{9,8},{10,11... | collective-permute-start | bytes 1572872 | tf_op jit(solution)/shard_map/ppermute | solution.py:22
  150.6 28.4 %collective-permute-start.30 = (bf16[256,1024]{1,0:T(8,128)(2,1)S(1)}, bf16[256,1024]{1,0:T(8,128)(2,1)S(1)}, u32[]{:S(2)}, u32[]{:S(2)}) collective-permute-start(bf16[256,1024]{1,0:T(8,128)(2,1)S(1)} %fusion), channel_id=1, source_target_pairs={{0,2},{2,0},{1,3},{3,1},{4,6},{6,4},{5,7},{7,5},{8,10},{10,8},{9,1... | collective-permute-start | bytes 1572872 | tf_op jit(solution)/shard_map/ppermute | solution.py:22
  179.3 7.3 %collective-permute-start.31 = (bf16[256,1024]{1,0:T(8,128)(2,1)S(1)}, bf16[256,1024]{1,0:T(8,128)(2,1)S(1)}, u32[]{:S(2)}, u32[]{:S(2)}) collective-permute-start(bf16[256,1024]{1,0:T(8,128)(2,1)S(1)} %select_convert_fusion.mine_ref), channel_id=1, source_target_pairs={{0,1},{1,0},{2,3},{3,2},{4,5},{5,4},{6,7},{7,6},{8,9},{9,8},{10,11... | collective-permute-start | bytes 1572872 | tf_op jit(solution)/shard_map/ppermute | solution.py:22
  (14 other events, 108.0 us)

commit v4 on v3

--- a/solution.py
+++ b/solution.py
@@ -127,43 +127,49 @@
     )(spot, wide, bias, *weights)
 
 
-def decode_kernel(step, spot_ref, mine_ref, other_ref, weight_ref, out_ref, rows):
+def decode_kernel(steps, spot_ref, mine_ref, other_ref, weight_ref, *refs):
+    outs, rows = refs[:-1], refs[-1]
     core = spot_ref[0]
-    far = lax.rem(spot_ref[1] + step, RING)
-    nlayer, part, width = out_ref.shape[1:]
-
-    @pl.when(core == 0)
-    def _():
-        @pl.when(lax.rem(far, 2) == 0)
+    nlayer, part, width = outs[0].shape[1:]
+    block = RING * part
+    for index, step in enumerate(steps):
+        far = lax.rem(spot_ref[1] + step, RING)
+        first = index * block
+
+        @pl.when(core == 0)
         def _():
-            rows[...] = mine_ref[far // 2]
-
-        @pl.when(lax.rem(far, 2) == 1)
+            @pl.when(lax.rem(far, 2) == 0)
+            def _():
+                rows[pl.ds(first, block), :] = mine_ref[far // 2]
+
+            @pl.when(lax.rem(far, 2) == 1)
+            def _():
+                rows[pl.ds(first, block), :] = other_ref[far // 2]
+
+        @pl.when(core == 1)
         def _():
-            rows[...] = other_ref[far // 2]
-
-    @pl.when(core == 1)
-    def _():
-        for block in range(RING):
-            act_ref = mine_ref if block % 2 else other_ref
-            place = pl.ds(pl.multiple_of(far * part, part), part)
-            rows[pl.ds(block * part, part), :] = act_ref[block // 2, place, :]
+            for t in range(RING):
+                act_ref = mine_ref if t % 2 else other_ref
+                place = pl.ds(pl.multiple_of(far * part, part), part)
+                rows[pl.ds(first + t * part, part), :] = act_ref[t // 2, place, :]
 
     for write in range(nlayer):
         output = dot(rows[...], weight_ref[write], 1, 1).astype(jnp.bfloat16)
-        out_ref[:, write] = output.reshape(RING, part, width)
-
-
-def decode(step, spot, mine, other, weight, part):
+        for index, out_ref in enumerate(outs):
+            piece = output[index * block : (index + 1) * block]
+            out_ref[:, write] = piece.reshape(RING, part, width)
+
+
+def decode(steps, spot, mine, other, weight, part):
     few, feats = mine.shape
     nlayer, width, _ = weight.shape
     whole = pl.BlockSpec(memory_space=pltpu.VMEM)
     return pl.pallas_call(
-        functools.partial(decode_kernel, step),
+        functools.partial(decode_kernel, steps),
         in_specs=[pl.BlockSpec(memory_space=pltpu.SMEM)] + [whole] * 3,
-        out_specs=whole,
-        out_shape=jax.ShapeDtypeStruct((RING, nlayer, part, width), jnp.bfloat16),
-        scratch_shapes=[pltpu.VMEM((RING * part, feats), jnp.bfloat16)],
+        out_specs=[whole] * len(steps),
+        out_shape=[jax.ShapeDtypeStruct((RING, nlayer, part, width), jnp.bfloat16)] * len(steps),
+        scratch_shapes=[pltpu.VMEM((len(steps) * RING * part, feats), jnp.bfloat16)],
         compiler_params=pltpu.CompilerParams(vmem_limit_bytes=GRANT),
     )(spot, mine.reshape(2, few // 2, feats), other.reshape(2, few // 2, feats), weight)
 
@@ -222,9 +228,10 @@
     )(*pieces, weight)
 
 
-def back_kernel(spot_ref, low_ref, high_ref, weight_ref, near_ref, keep_ref, give_ref, total):
+def back_kernel(spot_ref, low_ref, high_ref, weight_ref, near_ref, *refs):
+    keeps, gives, total = refs[:2], refs[2:4], refs[4]
     core = spot_ref[0]
-    part = keep_ref.shape[2]
+    part, cols = keeps[0].shape[2:]
     for write in range(weight_ref.shape[0]):
         grad = jnp.concatenate([rows_of(low_ref, write), rows_of(high_ref, write)], axis=0)
         term = dot(grad, weight_ref[write], 1, 0)
@@ -239,11 +246,14 @@
 
         @pl.when(lax.rem(x, 2) == core)
         def _():
-            keep_ref[x // 2, y] = rows
+            for side in range(2):
+                keeps[side][x // 2, y] = rows[:, side * cols : (side + 1) * cols]
 
         @pl.when(lax.rem(x, 2) != core)
         def _():
-            give_ref[x // 2, y] = rows.astype(jnp.bfloat16)
+            for side in range(2):
+                piece = rows[:, side * cols : (side + 1) * cols]
+                gives[side][x // 2, y] = piece.astype(jnp.bfloat16)
 
     block = RING * part
     sources = ((near_ref, 0), (near_ref, block), (total, 0), (near_ref, 2 * block))
@@ -254,21 +264,20 @@
     low, high = far
     part = low.shape[2]
     feats = weight.shape[2]
-    shape = (2, RING, part, feats)
-    whole = pl.BlockSpec(memory_space=pltpu.VMEM)
-    keep, give = pl.pallas_call(
+    shape = (2, RING, part, feats // 2)
+    whole = pl.BlockSpec(memory_space=pltpu.VMEM)
+    parts = pl.pallas_call(
         back_kernel,
         in_specs=[pl.BlockSpec(memory_space=pltpu.SMEM)] + [whole] * 4,
-        out_specs=[whole] * 2,
-        out_shape=[
-            jax.ShapeDtypeStruct(shape, jnp.float32),
-            jax.ShapeDtypeStruct(shape, jnp.bfloat16),
-        ],
+        out_specs=[whole] * 4,
+        out_shape=[jax.ShapeDtypeStruct(shape, jnp.float32)] * 2
+        + [jax.ShapeDtypeStruct(shape, jnp.bfloat16)] * 2,
         scratch_shapes=[pltpu.VMEM((RING * part, feats), jnp.float32)],
         compiler_params=pltpu.CompilerParams(vmem_limit_bytes=GRANT),
         name="back",
     )(spot, low, high, weight, near)
-    return keep.reshape(-1, feats), give.reshape(-1, feats)
+    parts = [part.reshape(-1, feats // 2) for part in parts]
+    return parts[:2], parts[2:]
 
 
 def outer_kernel(spot_ref, mine_ref, other_ref, *refs):
@@ -330,7 +339,8 @@
     )(spot, mine, other, *pieces)
 
 
-def last_kernel(moved_ref, next_ref, mine_ref, other_ref, out_ref, bias_ref):
+def last_kernel(moved_ref, next_ref, mine_ref, other_ref, *refs):
+    out_ref, bias_ref = refs[-2:]
     mine, other = mine_ref[...], other_ref[...]
     total = dot(moved_ref[...], mine, 1, 0) + dot(next_ref[...], other, 1, 0)
     out_ref[...] = total.astype(jnp.bfloat16)
@@ -338,30 +348,32 @@
     bias_ref[...] = sums[0] + sums[1]
 
 
-def last(moved, moved_next, mine, other):
+def last(side, moved, moved_next, mine, other, before):
     width, few = moved.shape
-    feats = mine.shape[1]
-    cut = min(feats, 256)
+    cols = mine.shape[1]
+    cut = min(cols, 256)
+    first = side * (cols // cut)
     return pl.pallas_call(
         last_kernel,
-        grid=(feats // cut,),
+        grid=(cols // cut,),
         in_specs=[
             pl.BlockSpec((width, few), lambda n: (0, 0)),
             pl.BlockSpec((width, few), lambda n: (0, 0)),
             pl.BlockSpec((few, cut), lambda n: (0, n)),
             pl.BlockSpec((few, cut), lambda n: (0, n)),
-        ],
+        ]
+        + [pl.BlockSpec(memory_space=pl.ANY)] * len(before),
         out_specs=[
-            pl.BlockSpec((width, cut), lambda n: (0, n)),
-            pl.BlockSpec((1, cut), lambda n: (0, n)),
+            pl.BlockSpec((width, cut), lambda n: (0, first + n)),
+            pl.BlockSpec((1, cut), lambda n: (0, first + n)),
         ],
         out_shape=[
-            jax.ShapeDtypeStruct((width, feats), jnp.bfloat16),
-            jax.ShapeDtypeStruct((1, feats), jnp.float32),
+            jax.ShapeDtypeStruct((width, 2 * cols), jnp.bfloat16),
+            jax.ShapeDtypeStruct((1, 2 * cols), jnp.float32),
         ],
-        compiler_params=pltpu.CompilerParams(vmem_limit_bytes=GRANT),
-        name="last",
-    )(moved, moved_next, mine, other)
+        input_output_aliases={4 + k: k for k in range(len(before))},
+        compiler_params=pltpu.CompilerParams(vmem_limit_bytes=GRANT),
+    )(moved, moved_next, mine, other, *before)
 
 
 def step(captured, target, enc_weight, enc_bias, dec_weight, dec_bias):
@@ -408,9 +420,10 @@
 
     held = decoder
     taken = [None] * RING
-    for j in (2, 1, 3, 0):
-        part = decode(j, spot, act, act_next, held, target.shape[1])
-        taken[j] = turned(part, j, True) if j else part
+    for steps in ((2,), (1, 3), (0,)):
+        sums = decode(steps, spot, act, act_next, held, target.shape[1])
+        for j, part in zip(steps, sums):
+            taken[j] = turned(part, j, True) if j else part
     parts = halfway(spot, dec_bias, target[0], taken)
     recon = parts[0]
     for k in range(1, RING):
@@ -427,15 +440,22 @@
     around, before, far, after = forwarded(scaled.astype(jnp.bfloat16))
 
     near = near_rows((around, before, after), held)
-    keep, give = back(spot, far, held, near)
-    keep = keep + swapped(give, "core").astype(jnp.float32)
-    keep = lax.optimization_barrier(keep.astype(jnp.bfloat16))
-    crossing = swapped(keep, "half")
-    grads, _ = lax.optimization_barrier(((around, before, *far, after), keep))
+    keeps, gives = back(spot, far, held, near)
+    crossings = []
+    for side in range(2):
+        keep = keeps[side] + swapped(gives[side], "core").astype(jnp.float32)
+        keeps[side] = lax.optimization_barrier(keep.astype(jnp.bfloat16))
+        crossings.append(swapped(keeps[side], "half"))
+    grads, _ = lax.optimization_barrier(((around, before, *far, after), keeps))
     dec_grads, dec_bias_grad = outer(spot, act, act_next, grads)
-    grad_mine = keep.astype(jnp.float32) + crossing.astype(jnp.float32)
-    grad_pre = jnp.where(act > 0, grad_mine, 0.0).astype(jnp.bfloat16)
-    enc_grad, enc_bias_grad = last(moved, moved_next, grad_pre, swapped(grad_pre, "core"))
+    results = ()
+    for side in range(2):
+        grad_mine = keeps[side].astype(jnp.float32) + crossings[side].astype(jnp.float32)
+        on = act[:, side * cols : (side + 1) * cols] > 0
+        grad_pre = jnp.where(on, grad_mine, 0.0).astype(jnp.bfloat16)
+        other = swapped(grad_pre, "core")
+        results = last(side, moved, moved_next, grad_pre, other, results)
+    enc_grad, enc_bias_grad = results
     return (enc_grad[None], enc_bias_grad, dec_grads.swapaxes(1, 2)[None], dec_bias_grad)
 
 

time: 189 us -> 185 us (0.979)
  waiting for transfers between devices: 93.4 us -> 89.6 us
  Pallas kernels: 25.6 us -> 23.5 us
    ppermute x10 -> x13, waiting for transfers between devices: 36.5 us -> 33.5 us  [swapped(): return lax.ppermute(value, axis, [(0, 1), (1, 0)])]
    pallas_call x5, Pallas kernels: 11.9 us -> 9.89 us  [the longest x3 7.01 us: decode(): pl.pallas_call(functools.partial(decode_kernel, steps), in_specs=[pl.Bloc...]
    ppermute x10 -> x13, starting transfers between devices: 34.8 us -> 35.6 us  [swapped(): return lax.ppermute(value, axis, [(0, 1), (1, 0)])]
  transfers between devices with their start and end apart: 32 -> 35, of which waited for: 23 -> 24; matrix products, arithmetic and copies ran while one was open for 0% -> 0% of each run, Pallas kernels for 6% -> 7%
where the time goes in v4:
time: 185 us
  waiting for transfers between devices  89.6 us (48%)
  starting transfers between devices  68.4 us (37%)
  Pallas kernels  23.5 us (13%)
    ppermute x19, waiting for transfers between devices, turned(): return lax.ppermute(value, ALL, pairs)  51.1 us
    ppermute x13, starting transfers between devices, swapped(): return lax.ppermute(value, axis, [(0, 1), (1, 0)])  35.6 us
    ppermute x13, waiting for transfers between devices, swapped(): return lax.ppermute(value, axis, [(0, 1), (1, 0)])  33.5 us
    ppermute x19, starting transfers between devices, turned(): return lax.ppermute(value, ALL, pairs)  22.7 us
    ppermute x3, starting transfers between devices, step(): taken = lax.ppermute(shared[least:], 'layer', ring).astype(jnp.float32)  10.1 us
    pallas_call x3, Pallas kernels, decode(): pl.pallas_call(functools.partial(decode_kernel, steps), in_specs=[pl.Bloc...  7.01 us
    pallas_call x1, Pallas kernels, outer(): pl.pallas_call(outer_kernel, grid_spec=pltpu.PrefetchScalarGridSpec(num_s...  5.91 us
    ppermute x3, waiting for transfers between devices, step(): taken = lax.ppermute(shared[least:], 'layer', ring).astype(jnp.float32)  5.01 us
  transfers between devices with their start and end apart: 35, of which 24 were waited for; matrix products, arithmetic and copies ran while one was open for 0% of the time, Pallas kernels for 7%

profile of v4, /device:TPU:1, one launch (start us, length us, event | category | flops | bytes accessed | tf_op | source)
XLA Modules:
  0.0 184.9 jit_solution(16853823503080655177)
XLA Ops:
  2.0 7.8 %collective-permute-start = (bf16[144,128]{1,0:T(8,128)(2,1)S(1)}, bf16[144,128]{1,0:T(8,128)(2,1)S(1)}, u32[]{:S(2)}, u32[]{:S(2)}) collective-permute-start(bf16[144,128]{1,0:T(8,128)(2,1)S(1)} %bitcast.74), channel_id=1, source_target_pairs={{0,2},{2,0},{1,3},{3,1},{4,6},{6,4},{5,7},{7,5},{8,10},{10,8},{9,1... | collective-permute-start | bytes 110600 | tf_op jit(solution)/shard_map/ppermute | solution.py:22
  11.2 2.6 %collective-permute-start.3 = (bf16[144,256]{1,0:T(8,128)(2,1)S(1)}, bf16[144,256]{1,0:T(8,128)(2,1)S(1)}, u32[]{:S(2)}, u32[]{:S(2)}) collective-permute-start(bf16[144,256]{1,0:T(8,128)(2,1)S(1)} %pad_maximum_fusion.3), channel_id=1, source_target_pairs={{0,48},{1,193},{2,50},{3,195},{4,52},{5,197},{6,54},{7,199},{8,56}... | collective-permute-start | bytes 221192 | tf_op jit(solution)/shard_map/ppermute | solution.py:42
  15.1 3.6 %collective-permute-done.2 = bf16[144,256]{1,0:T(8,128)(2,1)S(1)} collective-permute-done((bf16[144,256]{1,0:T(8,128)(2,1)S(1)}, bf16[144,256]{1,0:T(8,128)(2,1)S(1)}, u32[]{:S(2)}, u32[]{:S(2)}) %collective-permute-start.2) | collective-permute-done | bytes 73760 | tf_op jit(solution)/shard_map/ppermute | solution.py:42
  19.6 2.8 %collective-permute-start.6 = (bf16[4,144,256]{2,1,0:T(8,128)(2,1)S(1)}, bf16[4,144,256]{2,1,0:T(8,128)(2,1)S(1)}, u32[]{:S(2)}, u32[]{:S(2)}) collective-permute-start(bf16[4,144,256]{2,1,0:T(8,128)(2,1)S(1)} %pad_maximum_fusion.2.refs_0_), channel_id=1, source_target_pairs={{0,192},{1,49},{2,194},{3,51},{4,196},{5,53},{6,198},{7,55},{8,200... | collective-permute-start | bytes 884744 | tf_op jit(solution)/shard_map/ppermute | solution.py:42
  23.4 5.8 %collective-permute-done.6.refs_3_ = bf16[4,144,256]{2,1,0:T(8,128)(2,1)S(1)} collective-permute-done((bf16[4,144,256]{2,1,0:T(8,128)(2,1)S(1)}, bf16[4,144,256]{2,1,0:T(8,128)(2,1)S(1)}, u32[]{:S(2)}, u32[]{:S(2)}) %collective-permute-start.6) | collective-permute-done | bytes 294944 | tf_op jit(solution)/shard_map/ppermute | solution.py:42
  29.8 3.1 %collective-permute-done.4.refs_1_ = bf16[4,144,256]{2,1,0:T(8,128)(2,1)S(1)} collective-permute-done((bf16[4,144,256]{2,1,0:T(8,128)(2,1)S(1)}, bf16[4,144,256]{2,1,0:T(8,128)(2,1)S(1)}, u32[]{:S(2)}, u32[]{:S(2)}) %collective-permute-start.4) | collective-permute-done | bytes 294944 | tf_op jit(solution)/shard_map/ppermute | solution.py:42
  33.6 3.9 %collective-permute-start.8 = (bf16[576,512]{1,0:T(8,128)(2,1)S(1)}, bf16[576,512]{1,0:T(8,128)(2,1)S(1)}, u32[]{:S(2)}, u32[]{:S(2)}) collective-permute-start(bf16[576,512]{1,0:T(8,128)(2,1)S(1)} %collective-permute-done.7.refs_2_), channel_id=1, source_target_pairs={{0,1},{1,0},{2,3},{3,2},{4,5},{5,4},{6,7},{7,6},{8,9},{9,8},{10,11... | collective-permute-start | bytes 1769480 | tf_op jit(solution)/shard_map/ppermute | solution.py:22
  42.0 6.1 %collective-permute-start.11 = (bf16[256,512]{1,0:T(8,128)(2,1)S(1)}, bf16[256,512]{1,0:T(8,128)(2,1)S(1)}, u32[]{:S(2)}, u32[]{:S(2)}) collective-permute-start(bf16[256,512]{1,0:T(8,128)(2,1)S(1)} %encode.1), channel_id=1, source_target_pairs={{0,2},{2,0},{1,3},{3,1},{4,6},{6,4},{5,7},{7,5},{8,10},{10,8},{9,1... | collective-permute-start | bytes 786440 | tf_op jit(solution)/shard_map/ppermute | solution.py:22
  48.1 6.3 %collective-permute-done.11 = bf16[256,512]{1,0:T(8,128)(2,1)S(1)} collective-permute-done((bf16[256,512]{1,0:T(8,128)(2,1)S(1)}, bf16[256,512]{1,0:T(8,128)(2,1)S(1)}, u32[]{:S(2)}, u32[]{:S(2)}) %collective-permute-start.11) | collective-permute-done | bytes 262176 | tf_op jit(solution)/shard_map/ppermute | solution.py:22
  63.1 2.7 %collective-permute-start.15 = (bf16[4,4,32,576]{3,2,1,0:T(8,128)(2,1)S(1)}, bf16[4,4,32,576]{3,2,1,0:T(8,128)(2,1)S(1)}, u32[]{:S(2)}, u32[]{:S(2)}) collective-permute-start(bf16[4,4,32,576]{3,2,1,0:T(8,128)(2,1)S(1)} %get-tuple-element.50), channel_id=1, source_target_pairs={{0,192},{1,49},{2,194},{3,51},{4,196},{5,53},{6,198},{7,55},{8,200... | collective-permute-start | bytes 1769480 | tf_op jit(solution)/shard_map/ppermute | solution.py:42
  68.0 5.3 %collective-permute-done.14.refs_2_ = bf16[4,4,32,576]{3,2,1,0:T(8,128)(2,1)S(1)} collective-permute-done((bf16[4,4,32,576]{3,2,1,0:T(8,128)(2,1)S(1)}, bf16[4,4,32,576]{3,2,1,0:T(8,128)(2,1)S(1)}, u32[]{:S(2)}, u32[]{:S(2)}) %collective-permute-start.14) | collective-permute-done | bytes 589856 | tf_op jit(solution)/shard_map/ppermute | solution.py:42
  73.4 7.0 %collective-permute-done.13.refs_1_ = bf16[4,4,32,576]{3,2,1,0:T(8,128)(2,1)S(1)} collective-permute-done((bf16[4,4,32,576]{3,2,1,0:T(8,128)(2,1)S(1)}, bf16[4,4,32,576]{3,2,1,0:T(8,128)(2,1)S(1)}, u32[]{:S(2)}, u32[]{:S(2)}) %collective-permute-start.13) | collective-permute-done | bytes 589856 | tf_op jit(solution)/shard_map/ppermute | solution.py:42
  84.2 4.7 %collective-permute-done.16 = bf16[4,32,576]{2,1,0:T(8,128)(2,1)S(1)} collective-permute-done((bf16[4,32,576]{2,1,0:T(8,128)(2,1)S(1)}, bf16[4,32,576]{2,1,0:T(8,128)(2,1)S(1)}, u32[]{:S(2)}, u32[]{:S(2)}) %collective-permute-start.16) | collective-permute-done | bytes 147488 | tf_op jit(solution)/shard_map/ppermute | solution.py:42
  92.1 5.7 %collective-permute-start.19 = (bf16[3,32,576]{2,1,0:T(8,128)(2,1)S(1)}, bf16[3,32,576]{2,1,0:T(8,128)(2,1)S(1)}, u32[]{:S(2)}, u32[]{:S(2)}) collective-permute-start(bf16[3,32,576]{2,1,0:T(8,128)(2,1)S(1)} %slice.19), channel_id=1, source_target_pairs={{0,4},{4,8},{8,12},{12,0},{1,5},{5,9},{9,13},{13,1},{2,6},{6,10},{... | collective-permute-start | bytes 331784 | tf_op jit(solution)/shard_map/ppermute | solution.py:437
  99.8 5.0 %collective-permute-done.20 = bf16[2,32,576]{2,1,0:T(8,128)(2,1)S(1)} collective-permute-done((bf16[2,32,576]{2,1,0:T(8,128)(2,1)S(1)}, bf16[2,32,576]{2,1,0:T(8,128)(2,1)S(1)}, u32[]{:S(2)}, u32[]{:S(2)}) %collective-permute-start.20) | collective-permute-done | bytes 73760 | tf_op jit(solution)/shard_map/ppermute | solution.py:437
  105.0 4.5 %collective-permute-start.24 = (bf16[4,32,576]{2,1,0:T(8,128)(2,1)S(1)}, bf16[4,32,576]{2,1,0:T(8,128)(2,1)S(1)}, u32[]{:S(2)}, u32[]{:S(2)}) collective-permute-start(bf16[4,32,576]{2,1,0:T(8,128)(2,1)S(1)} %select_convert_fusion.2), channel_id=1, source_target_pairs={{0,48},{1,193},{2,50},{3,195},{4,52},{5,197},{6,54},{7,199},{8,56}... | collective-permute-start | bytes 442376 | tf_op jit(solution)/shard_map/ppermute | solution.py:42
  110.1 3.3 %collective-permute-done.24 = bf16[4,32,576]{2,1,0:T(8,128)(2,1)S(1)} collective-permute-done((bf16[4,32,576]{2,1,0:T(8,128)(2,1)S(1)}, bf16[4,32,576]{2,1,0:T(8,128)(2,1)S(1)}, u32[]{:S(2)}, u32[]{:S(2)}) %collective-permute-start.24) | collective-permute-done | bytes 147488 | tf_op jit(solution)/shard_map/ppermute | solution.py:42
  118.5 8.3 %collective-permute-done.27.refs_2_.refs_4_ = bf16[4,4,32,576]{3,2,1,0:T(8,128)(2,1)S(1)} collective-permute-done((bf16[4,4,32,576]{3,2,1,0:T(8,128)(2,1)S(1)}, bf16[4,4,32,576]{3,2,1,0:T(8,128)(2,1)S(1)}, u32[]{:S(2)}, u32[]{:S(2)}) %collective-permute-start.27) | collective-permute-done | bytes 589856 | tf_op jit(solution)/shard_map/ppermute | solution.py:42
  128.7 2.6 %near.1.near_ref = f32[384,1024]{1,0:T(8,128)S(1)} custom-call(bf16[4,4,32,576]{3,2,1,0:T(8,128)(2,1)S(1)} %pad_maximum_fusion.refs_0_, bf16[4,4,32,576]{3,2,1,0:T(8,128)(2,1)S(1)} %collective-permute-done.25.refs_1_, bf16[4,4,32,576]{3,2,1,0:T(8,128)(2,1)S(1)} %collective-permute-done.27.refs_2_.refs_4_, bf16[4,576,1024]{2,1,0:T(8,128)(2,1)S(1)} %bitcast.49), custom_call_target="tpu_custom_call" | custom-call | tf_op jit(solution)/shard_map/near/pallas_call | solution.py:221
  137.5 6.8 %collective-permute-start.32 = (bf16[256,512]{1,0:T(8,128)(2,1)S(1)}, bf16[256,512]{1,0:T(8,128)(2,1)S(1)}, u32[]{:S(2)}, u32[]{:S(2)}) collective-permute-start(bf16[256,512]{1,0:T(8,128)(2,1)S(1)} %bitcast.64), channel_id=1, source_target_pairs={{0,1},{1,0},{2,3},{3,2},{4,5},{5,4},{6,7},{7,6},{8,9},{9,8},{10,11... | collective-permute-start | bytes 786440 | tf_op jit(solution)/shard_map/ppermute | solution.py:22
  145.5 6.2 %collective-permute-start.33 = (bf16[256,512]{1,0:T(8,128)(2,1)S(1)}, bf16[256,512]{1,0:T(8,128)(2,1)S(1)}, u32[]{:S(2)}, u32[]{:S(2)}) collective-permute-start(bf16[256,512]{1,0:T(8,128)(2,1)S(1)} %fusion), channel_id=1, source_target_pairs={{0,2},{2,0},{1,3},{3,1},{4,6},{6,4},{5,7},{7,5},{8,10},{10,8},{9,1... | collective-permute-start | bytes 786440 | tf_op jit(solution)/shard_map/ppermute | solution.py:22
  152.0 17.2 %collective-permute-done.33 = bf16[256,512]{1,0:T(8,128)(2,1)S(1)} collective-permute-done((bf16[256,512]{1,0:T(8,128)(2,1)S(1)}, bf16[256,512]{1,0:T(8,128)(2,1)S(1)}, u32[]{:S(2)}, u32[]{:S(2)}) %collective-permute-start.33) | collective-permute-done | bytes 262176 | tf_op jit(solution)/shard_map/ppermute | solution.py:22
  171.0 3.8 %collective-permute-done.30 = bf16[256,512]{1,0:T(8,128)(2,1)S(1)} collective-permute-done((bf16[256,512]{1,0:T(8,128)(2,1)S(1)}, bf16[256,512]{1,0:T(8,128)(2,1)S(1)}, u32[]{:S(2)}, u32[]{:S(2)}) %collective-permute-start.30) | collective-permute-done | bytes 262176 | tf_op jit(solution)/shard_map/ppermute | solution.py:22
  176.1 5.9 %outer.1 = (bf16[4,576,1024]{2,1,0:T(8,128)(2,1)}, f32[1,576]{1,0:T(1,128)}) custom-call(s32[5]{0:T(128)S(1)} %stack.53.spot_ref, bf16[256,1024]{1,0:T(8,128)(2,1)S(1)} %pad_maximum_fusion.1.mine_ref, bf16[256,1024]{1,0:T(8,128)(2,1)S(1)} %collective-permute-done.12.other_ref, bf16[4,4,32,576]{3,2,1,0:T(8,128)(2,1)S(1)} %pad_maximum_fusion.refs_0_, ...), custom_call_target="tpu_custom_call" | custom-call | flops 2415919104 | bytes 4718592 | tf_op jit(solution)/shard_map/outer/pallas_call | solution.py:309
  (89 shorter events, 53.1 us)
Async XLA Ops:
  2.0 9.1 %collective-permute-start = (bf16[144,128]{1,0:T(8,128)(2,1)S(1)}, bf16[144,128]{1,0:T(8,128)(2,1)S(1)}, u32[]{:S(2)}, u32[]{:S(2)}) collective-permute-start(bf16[144,128]{1,0:T(8,128)(2,1)S(1)} %bitcast.74), channel_id=1, source_target_pairs={{0,2},{2,0},{1,3},{3,1},{4,6},{6,4},{5,7},{7,5},{8,10},{10,8},{9,1... | collective-permute-start | bytes 110600 | tf_op jit(solution)/shard_map/ppermute | solution.py:22
  9.8 23.8 %collective-permute-start.7 = (bf16[576,512]{1,0:T(8,128)(2,1)S(1)}, bf16[576,512]{1,0:T(8,128)(2,1)S(1)}, u32[]{:S(2)}, u32[]{:S(2)}) collective-permute-start(bf16[576,512]{1,0:T(8,128)(2,1)S(1)} %dynamic-slice_bitcast_fusion), channel_id=1, source_target_pairs={{0,2},{2,0},{1,3},{3,1},{4,6},{6,4},{5,7},{7,5},{8,10},{10,8},{9,1... | collective-permute-start | bytes 1769480 | tf_op jit(solution)/shard_map/ppermute | solution.py:22
  19.6 9.6 %collective-permute-start.6 = (bf16[4,144,256]{2,1,0:T(8,128)(2,1)S(1)}, bf16[4,144,256]{2,1,0:T(8,128)(2,1)S(1)}, u32[]{:S(2)}, u32[]{:S(2)}) collective-permute-start(bf16[4,144,256]{2,1,0:T(8,128)(2,1)S(1)} %pad_maximum_fusion.2.refs_0_), channel_id=1, source_target_pairs={{0,192},{1,49},{2,194},{3,51},{4,196},{5,53},{6,198},{7,55},{8,200... | collective-permute-start | bytes 884744 | tf_op jit(solution)/shard_map/ppermute | solution.py:42
  22.4 7.4 %collective-permute-start.5 = (bf16[4,144,256]{2,1,0:T(8,128)(2,1)S(1)}, bf16[4,144,256]{2,1,0:T(8,128)(2,1)S(1)}, u32[]{:S(2)}, u32[]{:S(2)}) collective-permute-start(bf16[4,144,256]{2,1,0:T(8,128)(2,1)S(1)} %pad_maximum_fusion.2.refs_0_), channel_id=1, source_target_pairs={{0,128},{1,33},{2,130},{3,35},{4,132},{5,37},{6,134},{7,39},{8,136... | collective-permute-start | bytes 884744 | tf_op jit(solution)/shard_map/ppermute | solution.py:42
  22.7 10.2 %collective-permute-start.4 = (bf16[4,144,256]{2,1,0:T(8,128)(2,1)S(1)}, bf16[4,144,256]{2,1,0:T(8,128)(2,1)S(1)}, u32[]{:S(2)}, u32[]{:S(2)}) collective-permute-start(bf16[4,144,256]{2,1,0:T(8,128)(2,1)S(1)} %pad_maximum_fusion.2.refs_0_), channel_id=1, source_target_pairs={{0,64},{1,17},{2,66},{3,19},{4,68},{5,21},{6,70},{7,23},{8,72},{9,... | collective-permute-start | bytes 884744 | tf_op jit(solution)/shard_map/ppermute | solution.py:42
  42.0 12.4 %collective-permute-start.11 = (bf16[256,512]{1,0:T(8,128)(2,1)S(1)}, bf16[256,512]{1,0:T(8,128)(2,1)S(1)}, u32[]{:S(2)}, u32[]{:S(2)}) collective-permute-start(bf16[256,512]{1,0:T(8,128)(2,1)S(1)} %encode.1), channel_id=1, source_target_pairs={{0,2},{2,0},{1,3},{3,1},{4,6},{6,4},{5,7},{7,5},{8,10},{10,8},{9,1... | collective-permute-start | bytes 786440 | tf_op jit(solution)/shard_map/ppermute | solution.py:22
  61.8 11.5 %collective-permute-start.14 = (bf16[4,4,32,576]{3,2,1,0:T(8,128)(2,1)S(1)}, bf16[4,4,32,576]{3,2,1,0:T(8,128)(2,1)S(1)}, u32[]{:S(2)}, u32[]{:S(2)}) collective-permute-start(bf16[4,4,32,576]{3,2,1,0:T(8,128)(2,1)S(1)} %shard_map.95), channel_id=1, source_target_pairs={{0,128},{1,33},{2,130},{3,35},{4,132},{5,37},{6,134},{7,39},{8,136... | collective-permute-start | bytes 1769480 | tf_op jit(solution)/shard_map/ppermute | solution.py:42
  63.1 17.3 %collective-permute-start.13 = (bf16[4,4,32,576]{3,2,1,0:T(8,128)(2,1)S(1)}, bf16[4,4,32,576]{3,2,1,0:T(8,128)(2,1)S(1)}, u32[]{:S(2)}, u32[]{:S(2)}) collective-permute-start(bf16[4,4,32,576]{3,2,1,0:T(8,128)(2,1)S(1)} %get-tuple-element.49), channel_id=1, source_target_pairs={{0,64},{1,17},{2,66},{3,19},{4,68},{5,21},{6,70},{7,23},{8,72},{9,... | collective-permute-start | bytes 1769480 | tf_op jit(solution)/shard_map/ppermute | solution.py:42
  63.1 17.3 %collective-permute-start.15 = (bf16[4,4,32,576]{3,2,1,0:T(8,128)(2,1)S(1)}, bf16[4,4,32,576]{3,2,1,0:T(8,128)(2,1)S(1)}, u32[]{:S(2)}, u32[]{:S(2)}) collective-permute-start(bf16[4,4,32,576]{3,2,1,0:T(8,128)(2,1)S(1)} %get-tuple-element.50), channel_id=1, source_target_pairs={{0,192},{1,49},{2,194},{3,51},{4,196},{5,53},{6,198},{7,55},{8,200... | collective-permute-start | bytes 1769480 | tf_op jit(solution)/shard_map/ppermute | solution.py:42
  81.4 7.5 %collective-permute-start.16 = (bf16[4,32,576]{2,1,0:T(8,128)(2,1)S(1)}, bf16[4,32,576]{2,1,0:T(8,128)(2,1)S(1)}, u32[]{:S(2)}, u32[]{:S(2)}) collective-permute-start(bf16[4,32,576]{2,1,0:T(8,128)(2,1)S(1)} %get-tuple-element.52), channel_id=1, source_target_pairs={{0,16},{1,65},{2,18},{3,67},{4,20},{5,69},{6,22},{7,71},{8,24},{9,... | collective-permute-start | bytes 442376 | tf_op jit(solution)/shard_map/ppermute | solution.py:42
  81.5 7.4 %collective-permute-start.17 = (bf16[4,32,576]{2,1,0:T(8,128)(2,1)S(1)}, bf16[4,32,576]{2,1,0:T(8,128)(2,1)S(1)}, u32[]{:S(2)}, u32[]{:S(2)}) collective-permute-start(bf16[4,32,576]{2,1,0:T(8,128)(2,1)S(1)} %get-tuple-element.53), channel_id=1, source_target_pairs={{0,32},{1,129},{2,34},{3,131},{4,36},{5,133},{6,38},{7,135},{8,40}... | collective-permute-start | bytes 442376 | tf_op jit(solution)/shard_map/ppermute | solution.py:42
  89.7 15.1 %collective-permute-start.21 = (bf16[3,32,576]{2,1,0:T(8,128)(2,1)S(1)}, bf16[3,32,576]{2,1,0:T(8,128)(2,1)S(1)}, u32[]{:S(2)}, u32[]{:S(2)}) collective-permute-start(bf16[3,32,576]{2,1,0:T(8,128)(2,1)S(1)} %slice.19), channel_id=1, source_target_pairs={{0,12},{4,0},{8,4},{12,8},{1,13},{5,1},{9,5},{13,9},{2,14},{6,2},{... | collective-permute-start | bytes 331784 | tf_op jit(solution)/shard_map/ppermute | solution.py:437
  92.1 12.6 %collective-permute-start.19 = (bf16[3,32,576]{2,1,0:T(8,128)(2,1)S(1)}, bf16[3,32,576]{2,1,0:T(8,128)(2,1)S(1)}, u32[]{:S(2)}, u32[]{:S(2)}) collective-permute-start(bf16[3,32,576]{2,1,0:T(8,128)(2,1)S(1)} %slice.19), channel_id=1, source_target_pairs={{0,4},{4,8},{8,12},{12,0},{1,5},{5,9},{9,13},{13,1},{2,6},{6,10},{... | collective-permute-start | bytes 331784 | tf_op jit(solution)/shard_map/ppermute | solution.py:437
  105.0 8.5 %collective-permute-start.24 = (bf16[4,32,576]{2,1,0:T(8,128)(2,1)S(1)}, bf16[4,32,576]{2,1,0:T(8,128)(2,1)S(1)}, u32[]{:S(2)}, u32[]{:S(2)}) collective-permute-start(bf16[4,32,576]{2,1,0:T(8,128)(2,1)S(1)} %select_convert_fusion.2), channel_id=1, source_target_pairs={{0,48},{1,193},{2,50},{3,195},{4,52},{5,197},{6,54},{7,199},{8,56}... | collective-permute-start | bytes 442376 | tf_op jit(solution)/shard_map/ppermute | solution.py:42
  109.4 7.4 %collective-permute-start.22 = (bf16[4,32,576]{2,1,0:T(8,128)(2,1)S(1)}, bf16[4,32,576]{2,1,0:T(8,128)(2,1)S(1)}, u32[]{:S(2)}, u32[]{:S(2)}) collective-permute-start(bf16[4,32,576]{2,1,0:T(8,128)(2,1)S(1)} %select_convert_fusion.2), channel_id=1, source_target_pairs={{0,16},{1,65},{2,18},{3,67},{4,20},{5,69},{6,22},{7,71},{8,24},{9,... | collective-permute-start | bytes 442376 | tf_op jit(solution)/shard_map/ppermute | solution.py:42
  117.0 9.8 %collective-permute-start.27 = (bf16[4,4,32,576]{3,2,1,0:T(8,128)(2,1)S(1)}, bf16[4,4,32,576]{3,2,1,0:T(8,128)(2,1)S(1)}, u32[]{:S(2)}, u32[]{:S(2)}) collective-permute-start(bf16[4,4,32,576]{3,2,1,0:T(8,128)(2,1)S(1)} %pad_maximum_fusion.refs_0_), channel_id=1, source_target_pairs={{0,192},{1,49},{2,194},{3,51},{4,196},{5,53},{6,198},{7,55},{8,200... | collective-permute-start | bytes 1769480 | tf_op jit(solution)/shard_map/ppermute | solution.py:42
  117.1 11.3 %collective-permute-start.25 = (bf16[4,4,32,576]{3,2,1,0:T(8,128)(2,1)S(1)}, bf16[4,4,32,576]{3,2,1,0:T(8,128)(2,1)S(1)}, u32[]{:S(2)}, u32[]{:S(2)}) collective-permute-start(bf16[4,4,32,576]{3,2,1,0:T(8,128)(2,1)S(1)} %pad_maximum_fusion.refs_0_), channel_id=1, source_target_pairs={{0,64},{1,17},{2,66},{3,19},{4,68},{5,21},{6,70},{7,23},{8,72},{9,... | collective-permute-start | bytes 1769480 | tf_op jit(solution)/shard_map/ppermute | solution.py:42
  128.4 7.2 %collective-permute-start.26 = (bf16[2,4,32,576]{3,2,1,0:T(8,128)(2,1)S(1)}, bf16[2,4,32,576]{3,2,1,0:T(8,128)(2,1)S(1)}, u32[]{:S(2)}, u32[]{:S(2)}) collective-permute-start(bf16[2,4,32,576]{3,2,1,0:T(8,128)(2,1)S(1)} %slice.21), channel_id=1, source_target_pairs={{0,64},{1,17},{2,66},{3,19},{4,68},{5,21},{6,70},{7,23},{8,72},{9,... | collective-permute-start | bytes 884744 | tf_op jit(solution)/shard_map/ppermute | solution.py:42
  137.5 7.9 %collective-permute-start.32 = (bf16[256,512]{1,0:T(8,128)(2,1)S(1)}, bf16[256,512]{1,0:T(8,128)(2,1)S(1)}, u32[]{:S(2)}, u32[]{:S(2)}) collective-permute-start(bf16[256,512]{1,0:T(8,128)(2,1)S(1)} %bitcast.64), channel_id=1, source_target_pairs={{0,1},{1,0},{2,3},{3,2},{4,5},{5,4},{6,7},{7,6},{8,9},{9,8},{10,11... | collective-permute-start | bytes 786440 | tf_op jit(solution)/shard_map/ppermute | solution.py:22
  144.3 7.4 %collective-permute-start.29 = (bf16[256,512]{1,0:T(8,128)(2,1)S(1)}, bf16[256,512]{1,0:T(8,128)(2,1)S(1)}, u32[]{:S(2)}, u32[]{:S(2)}) collective-permute-start(bf16[256,512]{1,0:T(8,128)(2,1)S(1)} %bitcast.63), channel_id=1, source_target_pairs={{0,1},{1,0},{2,3},{3,2},{4,5},{5,4},{6,7},{7,6},{8,9},{9,8},{10,11... | collective-permute-start | bytes 786440 | tf_op jit(solution)/shard_map/ppermute | solution.py:22
  145.5 23.7 %collective-permute-start.33 = (bf16[256,512]{1,0:T(8,128)(2,1)S(1)}, bf16[256,512]{1,0:T(8,128)(2,1)S(1)}, u32[]{:S(2)}, u32[]{:S(2)}) collective-permute-start(bf16[256,512]{1,0:T(8,128)(2,1)S(1)} %fusion), channel_id=1, source_target_pairs={{0,2},{2,0},{1,3},{3,1},{4,6},{6,4},{5,7},{7,5},{8,10},{10,8},{9,1... | collective-permute-start | bytes 786440 | tf_op jit(solution)/shard_map/ppermute | solution.py:22
  151.7 23.1 %collective-permute-start.30 = (bf16[256,512]{1,0:T(8,128)(2,1)S(1)}, bf16[256,512]{1,0:T(8,128)(2,1)S(1)}, u32[]{:S(2)}, u32[]{:S(2)}) collective-permute-start(bf16[256,512]{1,0:T(8,128)(2,1)S(1)} %fusion.1), channel_id=1, source_target_pairs={{0,2},{2,0},{1,3},{3,1},{4,6},{6,4},{5,7},{7,5},{8,10},{10,8},{9,1... | collective-permute-start | bytes 786440 | tf_op jit(solution)/shard_map/ppermute | solution.py:22
  169.4 12.6 %collective-permute-start.34 = (bf16[256,512]{1,0:T(8,128)(2,1)S(1)}, bf16[256,512]{1,0:T(8,128)(2,1)S(1)}, u32[]{:S(2)}, u32[]{:S(2)}) collective-permute-start(bf16[256,512]{1,0:T(8,128)(2,1)S(1)} %select_convert_fusion.mine_ref), channel_id=1, source_target_pairs={{0,1},{1,0},{2,3},{3,2},{4,5},{5,4},{6,7},{7,6},{8,9},{9,8},{10,11... | collective-permute-start | bytes 786440 | tf_op jit(solution)/shard_map/ppermute | solution.py:22
  175.0 8.4 %collective-permute-start.31 = (bf16[256,512]{1,0:T(8,128)(2,1)S(1)}, bf16[256,512]{1,0:T(8,128)(2,1)S(1)}, u32[]{:S(2)}, u32[]{:S(2)}) collective-permute-start(bf16[256,512]{1,0:T(8,128)(2,1)S(1)} %select_convert_fusion.1.mine_ref), channel_id=1, source_target_pairs={{0,1},{1,0},{2,3},{3,2},{4,5},{5,4},{6,7},{7,6},{8,9},{9,8},{10,11... | collective-permute-start | bytes 786440 | tf_op jit(solution)/shard_map/ppermute | solution.py:22
  (17 other events, 125.7 us)
